TPU v7x, 32 devices: a whole 2x2x4 slice. The times are simulated.
32 devices in a mesh: tm: 8 (over z, y), roll: 4 (over x, core).
Axes of the slice: x: 2, y: 2, z: 4, core: 2. Of those that a mesh axis runs over, the one named last changes fastest.
Arguments:
- inputs: bfloat16 [4, 64, 32, 2048], P('roll', 'tm'), may hold values from -30 to 30
- cotangent: bfloat16 [4, 64, 32, 2048], P('roll', 'tm'), may hold values from -6 to 6
- memory_lists: int32 [4, 64, 8], P('roll', 'tm'), may hold values from -1 to 55, as said below
- w_query: bfloat16 [2048, 1024], replicated, may hold values from -1 to 1
- w_key: bfloat16 [2048, 1024], replicated, may hold values from -1 to 1
- w_value: bfloat16 [2048, 1024], replicated, may hold values from -0.125 to 0.125
- w_output: bfloat16 [1024, 2048], replicated, may hold values from -0.1875 to 0.1875
Outputs:
- attended: bfloat16 [4, 64, 32, 2048], P('roll', 'tm')
- grad_input: bfloat16 [4, 64, 32, 2048], P('roll', 'tm')
- grad_w_query: float32 [2048, 1024], P('tm')
- grad_w_key: float32 [2048, 1024], P('tm')
- grad_w_value: float32 [2048, 1024], P('tm')
- grad_w_output: float32 [1024, 2048], P('tm')
Inputs may be any that keep to these rules, and one draw needn't show every extreme that they name: `memory_lists`: every entry is -1 or a frame of the same rollout that lies in an earlier block of 8 frames and before frame f - 4. The frames named in one list differ, and -1 entries come after them. The frames of one block name at most 3 distinct frames of any other block, and exactly 3 of the block just before theirs.
All inputs are finite; a program needn't handle non-finite values.
Results may differ from a plain program's by a relative error of at most 0.02.
Values may be sent and summed in bfloat16 or wider, within the bound.
A program may use at most 192 MiB of HBM per device.

v0:
```python
import jax
import jax.numpy as jnp
from jax import lax
from jax.sharding import PartitionSpec as P

HEADS = 8
HEAD = 128
BAND = 4
MEM = 8
CAP = 3


masked_score = -1e30


def from_behind(block, axis, distance):
    devices = range(lax.axis_size(axis))
    route = [(i - distance, i) for i in devices if i - distance in devices]
    return lax.ppermute(block, axis, route)


def dot_last(left, right):
    return lax.dot_general(
        left, right, (((1,), (1,)), ((), ())), preferred_element_type=jnp.float32
    )


def dot_first(left, right):
    return lax.dot_general(
        left, right, (((0,), (0,)), ((), ())), preferred_element_type=jnp.float32
    )


def attend(queries, key_set, value_set, key_valid, grad_heads):
    frame_count, key_count, frame_tokens, inner_width = key_set.shape
    score_scale = HEAD ** (-0.5)
    query_h = queries.reshape(frame_count, frame_tokens, HEADS, HEAD)
    key_h = key_set.reshape(frame_count, key_count * frame_tokens, HEADS, HEAD)
    value_h = value_set.reshape(frame_count, key_count * frame_tokens, HEADS, HEAD)
    grad_h = grad_heads.reshape(frame_count, frame_tokens, HEADS, HEAD)
    scores = (
        jnp.einsum("fqhe,fkhe->fhqk", query_h, key_h, preferred_element_type=jnp.float32)
        * score_scale
    )
    key_mask = jnp.repeat(key_valid, frame_tokens, axis=1)[:, None, None, :]
    scores = jnp.where(key_mask, scores, masked_score)
    row_max = jnp.max(scores, axis=-1, keepdims=True)
    weights = jnp.exp(scores - row_max)
    weights = weights / jnp.sum(weights, axis=-1, keepdims=True)
    rounded = weights.astype(jnp.bfloat16)
    heads_out = jnp.einsum(
        "fhqk,fkhe->fqhe", rounded, value_h, preferred_element_type=jnp.float32
    ).astype(jnp.bfloat16)
    grad_prob = jnp.einsum("fqhe,fkhe->fhqk", grad_h, value_h, preferred_element_type=jnp.float32)
    row_dot = jnp.sum(weights * grad_prob, axis=-1, keepdims=True)
    dscore = (weights * (grad_prob - row_dot)).astype(jnp.bfloat16)
    grad_query = (
        jnp.einsum("fhqk,fkhe->fqhe", dscore, key_h, preferred_element_type=jnp.float32)
        * score_scale
    ).astype(jnp.bfloat16)
    grad_keys = (
        jnp.einsum("fhqk,fqhe->fkhe", dscore, query_h, preferred_element_type=jnp.float32)
        * score_scale
    )
    grad_values = jnp.einsum("fhqk,fqhe->fkhe", rounded, grad_h, preferred_element_type=jnp.float32)
    block_shape = (frame_count, key_count, frame_tokens, inner_width)
    return (
        heads_out.reshape(frame_count, frame_tokens, inner_width),
        grad_query.reshape(frame_count, frame_tokens, inner_width),
        grad_keys.reshape(block_shape),
        grad_values.reshape(block_shape),
    )


def spread_band(grad_band):
    frame_count, unused, frame_tokens, inner_width = grad_band.shape
    spread = jnp.zeros((frame_count + BAND, frame_tokens, inner_width), jnp.float32)
    for offset in range(BAND + 1):
        spread = spread + jnp.pad(grad_band[:, offset], ((offset, BAND - offset), (0, 0), (0, 0)))
    return spread


def slot_sum(hit_matrix, part):
    flat = part.reshape(part.shape[0] * part.shape[1], -1)
    high = flat.astype(jnp.bfloat16)
    low = (flat - high.astype(jnp.float32)).astype(jnp.bfloat16)
    return dot_first(hit_matrix, high) + dot_first(hit_matrix, low)


def local(inputs, cotangent, memory_lists, w_query, w_key, w_value, w_output):
    frame_count, frame_tokens, model_width = inputs.shape[1:]
    inner_width = w_query.shape[1]
    blocks = lax.axis_size("tm")
    position = lax.axis_index("tm")
    row_count = frame_count * frame_tokens
    flat_input = inputs.reshape(row_count, model_width)
    grad_flat = cotangent.reshape(row_count, model_width)
    queries = jnp.dot(flat_input, w_query, preferred_element_type=jnp.float32).astype(jnp.bfloat16)
    key_rows = jnp.dot(flat_input, w_key, preferred_element_type=jnp.float32).astype(jnp.bfloat16)
    value_rows = jnp.dot(flat_input, w_value, preferred_element_type=jnp.float32).astype(
        jnp.bfloat16
    )
    key_frames = key_rows.reshape(frame_count, frame_tokens, inner_width)
    value_frames = value_rows.reshape(frame_count, frame_tokens, inner_width)
    grad_heads = dot_last(grad_flat, w_output).astype(jnp.bfloat16)
    recalled = memory_lists[0]
    first_frame = position * frame_count
    last_frames = jnp.concatenate(
        [key_frames[frame_count - BAND :], value_frames[frame_count - BAND :]], axis=-1
    )
    before = from_behind(last_frames, "tm", 1)
    extended_keys = jnp.concatenate([before[..., :inner_width], key_frames], axis=0)
    extended_values = jnp.concatenate([before[..., inner_width:], value_frames], axis=0)
    band_keys = jnp.stack(
        [extended_keys[offset : offset + frame_count] for offset in range(BAND + 1)], axis=1
    )
    band_values = jnp.stack(
        [extended_values[offset : offset + frame_count] for offset in range(BAND + 1)], axis=1
    )
    band_index = (
        jnp.arange(frame_count, dtype=jnp.int32)[:, None]
        + jnp.arange(BAND + 1, dtype=jnp.int32)[None, :]
    )
    band_ok = first_frame + band_index - BAND >= 0
    all_lists = lax.all_gather(recalled, "tm", axis=0, tiled=True)
    targets = jnp.arange(blocks * frame_count, dtype=jnp.int32)
    wanted = jnp.any(recalled.reshape(-1, 1) == targets[None, :], axis=0).reshape(
        blocks, frame_count
    )
    slot_rank = jnp.cumsum(wanted.astype(jnp.int32), axis=1) - 1
    slot_table = (jnp.arange(blocks, dtype=jnp.int32)[:, None] * CAP + slot_rank).reshape(-1)
    mem_ok = recalled >= 0
    safe_ids = jnp.where(mem_ok, recalled, 0)
    slot_ids = jnp.where(mem_ok, slot_table[safe_ids], 0)
    own_frames = first_frame + jnp.arange(frame_count, dtype=jnp.int32)
    requested = jnp.any(
        all_lists.reshape(blocks, frame_count * MEM, 1) == own_frames[None, None, :], axis=1
    )
    asked_rank = jnp.cumsum(requested.astype(jnp.int32), axis=1) - 1
    picker = requested[:, None, :] & (
        asked_rank[:, None, :] == jnp.arange(CAP, dtype=jnp.int32)[None, :, None]
    )
    picker = picker.astype(jnp.bfloat16)
    out_keys = jnp.einsum(
        "bcp,pz->bcz", picker, key_rows.reshape(frame_count, -1), preferred_element_type=jnp.float32
    )
    out_values = jnp.einsum(
        "bcp,pz->bcz",
        picker,
        value_rows.reshape(frame_count, -1),
        preferred_element_type=jnp.float32,
    )
    piece_shape = (blocks, CAP, frame_tokens, inner_width)
    outgoing = jnp.concatenate(
        [
            out_keys.astype(jnp.bfloat16).reshape(piece_shape),
            out_values.astype(jnp.bfloat16).reshape(piece_shape),
        ],
        axis=-1,
    )
    incoming = lax.all_to_all(outgoing, "tm", split_axis=0, concat_axis=0, tiled=True)
    slot_rows = incoming.reshape(blocks * CAP, frame_tokens, 2 * inner_width)
    memory_keys = slot_rows[..., :inner_width][slot_ids]
    memory_values = slot_rows[..., inner_width:][slot_ids]
    key_set = jnp.concatenate([band_keys, memory_keys], axis=1)
    value_set = jnp.concatenate([band_values, memory_values], axis=1)
    key_valid = jnp.concatenate([band_ok, mem_ok], axis=1)
    heads_out, grad_query, grad_keys_all, grad_values_all = attend(
        queries.reshape(frame_count, frame_tokens, inner_width),
        key_set,
        value_set,
        key_valid,
        grad_heads.reshape(frame_count, frame_tokens, inner_width),
    )
    key_spread = spread_band(grad_keys_all[:, : BAND + 1])
    value_spread = spread_band(grad_values_all[:, : BAND + 1])
    rim = jnp.concatenate([key_spread[:BAND], value_spread[:BAND]], axis=-1).astype(jnp.bfloat16)
    passed = from_behind(rim, "tm", -1)
    passed_full = jnp.pad(passed.astype(jnp.float32), ((frame_count - BAND, 0), (0, 0), (0, 0)))
    slot_hits = (
        slot_ids.reshape(-1, 1) == jnp.arange(blocks * CAP, dtype=jnp.int32)[None, :]
    ) & mem_ok.reshape(-1, 1)
    hit_matrix = slot_hits.astype(jnp.bfloat16)
    slot_keys = (
        slot_sum(hit_matrix, grad_keys_all[:, BAND + 1 :]).astype(jnp.bfloat16).reshape(piece_shape)
    )
    slot_values = (
        slot_sum(hit_matrix, grad_values_all[:, BAND + 1 :])
        .astype(jnp.bfloat16)
        .reshape(piece_shape)
    )
    slot_grad = jnp.concatenate([slot_keys, slot_values], axis=-1)
    returned = lax.all_to_all(slot_grad, "tm", split_axis=0, concat_axis=0, tiled=True)
    gathered_back = jnp.einsum(
        "bcp,bcz->pz", picker, returned.reshape(blocks, CAP, -1), preferred_element_type=jnp.float32
    )
    gathered_back = gathered_back.reshape(frame_count, frame_tokens, 2 * inner_width)
    grad_keys = (
        key_spread[BAND:] + passed_full[..., :inner_width] + gathered_back[..., :inner_width]
    ).astype(jnp.bfloat16)
    grad_values = (
        value_spread[BAND:] + passed_full[..., inner_width:] + gathered_back[..., inner_width:]
    ).astype(jnp.bfloat16)
    grad_keys = grad_keys.reshape(row_count, inner_width)
    grad_values = grad_values.reshape(row_count, inner_width)
    query_rows = grad_query.reshape(row_count, inner_width)
    heads_rows = heads_out.reshape(row_count, inner_width)
    grad_input = (
        dot_last(query_rows, w_query) + dot_last(grad_keys, w_key) + dot_last(grad_values, w_value)
    )
    grad_input = grad_input.astype(jnp.bfloat16).reshape(1, frame_count, frame_tokens, model_width)
    attended = jnp.dot(heads_rows, w_output, preferred_element_type=jnp.float32).astype(
        jnp.bfloat16
    )
    attended = attended.reshape(1, frame_count, frame_tokens, model_width)
    partials = (
        dot_first(flat_input, query_rows).astype(jnp.bfloat16),
        dot_first(flat_input, grad_keys).astype(jnp.bfloat16),
        dot_first(flat_input, grad_values).astype(jnp.bfloat16),
        dot_first(heads_rows, grad_flat).astype(jnp.bfloat16),
    )
    shares = (
        lax.psum_scatter(partials[0], "tm", scatter_dimension=0, tiled=True).astype(jnp.float32),
        lax.psum_scatter(partials[1], "tm", scatter_dimension=0, tiled=True).astype(jnp.float32),
        lax.psum_scatter(partials[2], "tm", scatter_dimension=0, tiled=True).astype(jnp.float32),
        lax.psum_scatter(partials[3], "tm", scatter_dimension=0, tiled=True).astype(jnp.float32),
    )
    totals = (
        lax.psum(shares[0].astype(jnp.bfloat16), "roll").astype(jnp.float32),
        lax.psum(shares[1].astype(jnp.bfloat16), "roll").astype(jnp.float32),
        lax.psum(shares[2].astype(jnp.bfloat16), "roll").astype(jnp.float32),
        lax.psum(shares[3].astype(jnp.bfloat16), "roll").astype(jnp.float32),
    )
    return (attended, grad_input, totals[0], totals[1], totals[2], totals[3])


def solution(mesh):
    return jax.shard_map(
        local,
        mesh=mesh,
        in_specs=(
            P("roll", "tm", None, None),
            P("roll", "tm", None, None),
            P("roll", "tm", None),
            P(),
            P(),
            P(),
            P(),
        ),
        out_specs=(
            P("roll", "tm", None, None),
            P("roll", "tm", None, None),
            P("tm", None),
            P("tm", None),
            P("tm", None),
            P("tm", None),
        ),
        check_vma=False,
    )
```

profile of v0, /device:TPU:0, one launch (start us, length us, event | category | flops | bytes accessed | tf_op | source)
XLA Modules:
  0.0 683.3 jit_solution(1070487191711943485)
XLA Ops:
  7.2 32.7 %all-gather = s32[1,64,8]{2,1,0:T(8,128)S(1)} all-gather(s32[1,8,8]{2,1,0:T(8,128)} %param.9), channel_id=2, replica_groups=mesh['tm'=8,'roll'=4] {'tm'}, dimensions={1}, use_global_device_ids=true | all-gather | bytes 2304 | tf_op jit(solution)/shard_map/all_gather | solution.py:125
  40.6 3.6 convolution_convert_fusion.6
  50.9 5.6 all-to-all-start
  57.5 4.8 collective-permute-start
  70.2 19.8 %collective-permute-done = bf16[4,32,2048]{2,1,0:T(8,128)(2,1)} collective-permute-done((bf16[4,32,2048]{2,1,0:T(8,128)(2,1)}, bf16[4,32,2048]{2,1,0:T(8,128)(2,1)}, u32[]{:S(2)}, u32[]{:S(2)}) %collective-permute-start) | collective-permute-done | bytes 524320 | tf_op jit(solution)/shard_map/ppermute | solution.py:19
  99.3 21.9 %all-to-all-done = bf16[8,3,32,2048]{3,2,1,0:T(8,128)(2,1)} async-done(((bf16[8,3,32,2048]{3,2,1,0:T(8,128)(2,1)}), bf16[8,3,32,2048]{3,2,1,0:T(8,128)(2,1)}, u32[]{:S(2)}, u32[]{:S(2)}) %all-to-all-start) | async-done | bytes 3145760 | tf_op jit(solution)/shard_map/all_to_all | solution.py:161
  124.7 4.2 gather_fusion.2
  131.7 5.0 constant_dynamic-update-slice_fusion.2
  136.7 4.9 copy.180
  144.4 5.5 copy.179
  155.1 4.5 multiply_reduce_fusion
  168.1 5.8 fusion.42
  174.9 7.0 %convolution_bitcast_fusion = f32[8,416,8,128]{3,1,2,0:T(8,128)} fusion(bf16[8,32,8,128]{3,2,1,0:T(8,128)(2,1)S(1)} %bitcast.264, f32[8,8,32,416]{3,2,1,0:T(8,128)S(1)} %copy-done.3, f32[8,8,32]{2,1,0:T(8,128)S(1)} %get-tuple-element.50), kind=kOutput, calls=%fused_computation.15 | convolution fusion | flops 219807744 | bytes 17571840 | tf_op jit(solution)/shard_map/fhqk,fqhe->fkhe/dot_general | solution.py:65
  181.9 17.5 %copy.151 = f32[8,416,8,128]{3,2,1,0:T(8,128)} copy(f32[8,416,8,128]{3,1,2,0:T(8,128)} %convolution_bitcast_fusion) | data formatting | bytes 27262976 | tf_op jit(solution)/shard_map/fhqk,fqhe->fkhe/transpose | solution.py:65
  199.4 15.8 %reshape.193 = f32[8,13,32,1024]{3,2,1,0:T(8,128)} reshape(f32[8,416,8,128]{3,2,1,0:T(8,128)} %copy.151) | data formatting | bytes 27262976 | tf_op jit(solution)/shard_map/reshape | solution.py:71
  215.1 4.3 slice_bitcast_fusion
  219.4 5.0 copy.186
  228.3 6.3 multiply_bitcast_fusion
  234.6 17.5 %copy.144 = f32[8,416,8,128]{3,2,1,0:T(8,128)} copy(f32[8,416,8,128]{3,1,2,0:T(8,128)} %multiply_bitcast_fusion) | data formatting | bytes 27262976 | tf_op jit(solution)/shard_map/mul | solution.py:62
  252.1 16.0 %reshape.192 = f32[8,13,32,1024]{3,2,1,0:T(8,128)} reshape(f32[8,416,8,128]{3,2,1,0:T(8,128)} %copy.144) | data formatting | bytes 27262976 | tf_op jit(solution)/shard_map/reshape | solution.py:70
  271.6 4.3 slice_bitcast_fusion.1
  275.9 5.0 copy.184
  286.1 23.4 %all-to-all-start.1 = ((bf16[8,3,32,2048]{3,2,1,0:T(8,128)(2,1)}), bf16[8,3,32,2048]{3,2,1,0:T(8,128)(2,1)}, u32[]{:S(2)}, u32[]{:S(2)}) async-start(bf16[8,3,32,2048]{3,2,1,0:T(8,128)(2,1)} %pad_maximum_fusion.1), calls=%async_computation.1 | async-start | bytes 6291456 | tf_op jit(solution)/shard_map/all_to_all | solution.py:193
  327.6 21.7 %collective-permute-done.1 = bf16[4,32,2048]{2,0,1:T(4,128)(2,1)S(1)} collective-permute-done((bf16[4,32,2048]{2,0,1:T(4,128)(2,1)S(1)}, bf16[4,32,2048]{2,0,1:T(4,128)(2,1)S(1)}, u32[]{:S(2)}, u32[]{:S(2)}) %collective-permute-start.1) | collective-permute-done | bytes 524320 | tf_op jit(solution)/shard_map/ppermute | solution.py:19
  349.6 52.4 %all-to-all-done.1 = bf16[8,3,32,2048]{3,2,1,0:T(8,128)(2,1)} async-done(((bf16[8,3,32,2048]{3,2,1,0:T(8,128)(2,1)}), bf16[8,3,32,2048]{3,2,1,0:T(8,128)(2,1)}, u32[]{:S(2)}, u32[]{:S(2)}) %all-to-all-start.1) | async-done | bytes 3145760 | tf_op jit(solution)/shard_map/all_to_all | solution.py:193
  402.0 4.0 copy.157
  406.0 5.2 reshape.198
  423.5 4.5 convolution_convert_fusion.3
  431.0 92.4 %reduce-scatter.9.cloned.1.call-done = bf16[256,1024]{0,1:T(8,128)(2,1)} async-done(((bf16[2048,1024]{0,1:T(8,128)(2,1)}), bf16[256,1024]{0,1:T(8,128)(2,1)}) %reduce-scatter.9.cloned.1.call-update) | async-done | bytes 524304 | tf_op jit(solution)/shard_map/reduce_scatter | solution.py:225
  523.4 91.8 %reduce-scatter.7.cloned.1.call-done = bf16[256,1024]{0,1:T(8,128)(2,1)} async-done(((bf16[2048,1024]{0,1:T(8,128)(2,1)}), bf16[256,1024]{0,1:T(8,128)(2,1)}) %reduce-scatter.7.cloned.1.call-update) | async-done | bytes 524304 | tf_op jit(solution)/shard_map/reduce_scatter | solution.py:224
  615.3 3.6 fusion.68
  623.4 45.4 %all-reduce.14.cloned.1.call-done = (bf16[256,1024]{0,1:T(8,128)(2,1)}, bf16[256,1024]{0,1:T(8,128)(2,1)}, bf16[256,1024]{0,1:T(8,128)(2,1)}, bf16[128,2048]{1,0:T(8,128)(2,1)}) async-done(((bf16[256,1024]{0,1:T(8,128)(2,1)}, bf16[256,1024]{0,1:T(8,128)(2,1)}, bf16[256,1024]{0,1:T(8,128)(2,1)}, bf16[128,2048]{1,0:T(8,128)(2,1)}), (bf16[256,1024]{0,1:T(8,128)(2,1)}, bf16[256,1024]{0,1:T(8,128)(2,1)}, ...) | async-done | bytes 2097168 | tf_op jit(solution)/shard_map/psum | solution.py:229
  (179 shorter events, 107.1 us)
Async XLA Ops:
  7.2 33.4 %copy-start = (bf16[1,8,32,2048]{3,2,1,0:T(8,128)(2,1)S(1)}, bf16[1,8,32,2048]{3,2,1,0:T(8,128)(2,1)}, u32[]{:S(2)}) copy-start(bf16[1,8,32,2048]{3,2,1,0:T(8,128)(2,1)} %param.7) | copy-start | bytes 3145732
  40.3 7.2 %copy-start.27 = (pred[8,8]{0,1:T(8,128)(4,1)}, pred[8,8]{0,1:T(8,128)(4,1)S(1)}, u32[]{:S(2)}) copy-start(pred[8,8]{0,1:T(8,128)(4,1)S(1)} %copy.121) | copy-start | bytes 196
  40.6 6.9 %copy-start.25 = (s32[8,8]{0,1:T(8,128)}, s32[8,8]{0,1:T(8,128)S(1)}, u32[]{:S(2)}) copy-start(s32[8,8]{0,1:T(8,128)S(1)} %copy.122) | copy-start | bytes 772
  40.6 3.6 copy-start.12
  50.9 11.4 %copy-start.24 = (s32[1,8,8]{2,1,0:T(8,128)S(1)}, s32[1,8,8]{2,1,0:T(8,128)}, u32[]{:S(2)}) copy-start(s32[1,8,8]{2,1,0:T(8,128)} %param.9) | copy-start | bytes 772
  50.9 70.3 %all-to-all-start = ((bf16[8,3,32,2048]{3,2,1,0:T(8,128)(2,1)}), bf16[8,3,32,2048]{3,2,1,0:T(8,128)(2,1)}, u32[]{:S(2)}, u32[]{:S(2)}) async-start(bf16[8,3,32,2048]{3,2,1,0:T(8,128)(2,1)} %pad_maximum_fusion), calls=%async_computation | async-start | bytes 6291456 | tf_op jit(solution)/shard_map/all_to_all | solution.py:161
  56.6 371.5 %reduce-scatter.5.cloned.1.call-start = ((), (), s32[]{:S(2)}) async-start(), calls=%async_computation.6 | async-start | bytes 4718592 | tf_op jit(solution)/shard_map/reduce_scatter | solution.py:223
  57.5 32.6 %collective-permute-start = (bf16[4,32,2048]{2,1,0:T(8,128)(2,1)}, bf16[4,32,2048]{2,1,0:T(8,128)(2,1)}, u32[]{:S(2)}, u32[]{:S(2)}) collective-permute-start(bf16[4,32,2048]{2,1,0:T(8,128)(2,1)} %pad_maximum_fusion.4), channel_id=1, source_target_pairs={{0,4},{4,8},{8,12},{12,16},{16,20},{20,24},{24,28},{1,5},{5,9},{9,... | collective-permute-start | bytes 1572872 | tf_op jit(solution)/shard_map/ppermute | solution.py:19
  64.3 3.7 copy-start.21
  64.3 3.8 copy-start.29
  68.0 81.9 %copy-start.10 = (bf16[32,8,8,128]{3,2,1,0:T(8,128)(2,1)}, bf16[32,8,8,128]{3,2,1,0:T(8,128)(2,1)S(1)}, u32[]{:S(2)}) copy-start(bf16[32,8,8,128]{3,2,1,0:T(8,128)(2,1)S(1)} %copy.178) | copy-start | bytes 1572868
  136.7 4.9 copy-start.1
  141.6 13.5 %copy-start.4 = (bf16[416,8,8,128]{3,2,1,0:T(8,128)(2,1)}, bf16[416,8,8,128]{3,2,1,0:T(8,128)(2,1)S(1)}, u32[]{:S(2)}) copy-start(bf16[416,8,8,128]{3,2,1,0:T(8,128)(2,1)S(1)} %copy.180) | copy-start | bytes 20447236
  155.1 4.6 copy-start.2
  168.0 263.0 %reduce-scatter.11.cloned.1.call-start = ((), (), s32[]{:S(2)}) async-start(), calls=%async_computation.9 | async-start | bytes 4718592 | tf_op jit(solution)/shard_map/reduce_scatter | solution.py:226
  168.0 6.9 %copy-start.3 = (f32[8,8,32,416]{3,2,1,0:T(8,128)S(1)}, f32[8,8,32,416]{3,2,1,0:T(8,128)}, u32[]{:S(2)}) copy-start(f32[8,8,32,416]{3,2,1,0:T(8,128)} %copy-done.2) | copy-start | bytes 10223620
  168.1 6.9 %copy-start.20 = (bf16[32,8,8,128]{3,2,1,0:T(8,128)(2,1)S(1)}, bf16[32,8,8,128]{3,2,1,0:T(8,128)(2,1)}, u32[]{:S(2)}) copy-start(bf16[32,8,8,128]{3,2,1,0:T(8,128)(2,1)} %copy.182) | copy-start | bytes 1572868
  252.1 16.1 %copy-start.16 = (bf16[8,32,8,128]{3,2,1,0:T(8,128)(2,1)S(1)}, bf16[8,32,8,128]{3,2,1,0:T(8,128)(2,1)}, u32[]{:S(2)}) copy-start(bf16[8,32,8,128]{3,2,1,0:T(8,128)(2,1)} %copy.138) | copy-start | bytes 1572868
  252.1 16.1 %copy-start.22 = (bf16[1,8,32,2048]{3,2,1,0:T(8,128)(2,1)S(1)}, bf16[1,8,32,2048]{3,2,1,0:T(8,128)(2,1)}, u32[]{:S(2)}) copy-start(bf16[1,8,32,2048]{3,2,1,0:T(8,128)(2,1)} %param.8) | copy-start | bytes 3145732
  286.1 115.9 %all-to-all-start.1 = ((bf16[8,3,32,2048]{3,2,1,0:T(8,128)(2,1)}), bf16[8,3,32,2048]{3,2,1,0:T(8,128)(2,1)}, u32[]{:S(2)}, u32[]{:S(2)}) async-start(bf16[8,3,32,2048]{3,2,1,0:T(8,128)(2,1)} %pad_maximum_fusion.1), calls=%async_computation.1 | async-start | bytes 6291456 | tf_op jit(solution)/shard_map/all_to_all | solution.py:193
  309.5 214.0 %reduce-scatter.9.cloned.1.call-start = ((), (), s32[]{:S(2)}) async-start(), calls=%async_computation.8 | async-start | bytes 4718592 | tf_op jit(solution)/shard_map/reduce_scatter | solution.py:225
  326.1 23.2 %collective-permute-start.1 = (bf16[4,32,2048]{2,0,1:T(4,128)(2,1)S(1)}, bf16[4,32,2048]{2,0,1:T(4,128)(2,1)S(1)}, u32[]{:S(2)}, u32[]{:S(2)}) collective-permute-start(bf16[4,32,2048]{2,0,1:T(4,128)(2,1)S(1)} %pad_maximum_fusion.5), channel_id=1, source_target_pairs={{4,0},{8,4},{12,8},{16,12},{20,16},{24,20},{28,24},{5,1},{9,5},{13... | collective-permute-start | bytes 1572872 | tf_op jit(solution)/shard_map/ppermute | solution.py:19
  406.0 5.2 copy-start.26
  406.0 5.2 copy-start.28
  411.2 3.2 copy-start.9
  416.5 3.3 copy-start.18
  419.7 195.5 %reduce-scatter.7.cloned.1.call-start = ((), (), s32[]{:S(2)}) async-start(), calls=%async_computation.7 | async-start | bytes 4718592 | tf_op jit(solution)/shard_map/reduce_scatter | solution.py:224
  420.1 3.4 copy-start.17
  423.4 191.9 %copy-start.15 = (bf16[8,32,8,128]{3,2,1,0:T(8,128)(2,1)S(1)}, bf16[8,32,8,128]{3,2,1,0:T(8,128)(2,1)}, u32[]{:S(2)}) copy-start(bf16[8,32,8,128]{3,2,1,0:T(8,128)(2,1)} %copy-done.14) | copy-start | bytes 1572868
  423.4 245.3 %all-reduce.14.cloned.1.call-start = ((), (), s32[]{:S(2)}) async-start(), calls=%async_computation.10 | async-start | bytes 4194304 | tf_op jit(solution)/shard_map/psum | solution.py:229
  615.3 3.7 copy-start.13
  668.8 6.7 copy-start.23
  (8 other events, 15.8 us)
Sparse Core Ops, SparseCore 0:
  168.1 107.1 reduce-scatter.4
  278.9 152.0 reduce-scatter.10
  434.6 88.7 reduce-scatter.8
  526.9 88.3 reduce-scatter.6
  617.7 51.0 all-reduce.13
where the time goes:
time: 690 us; the launch traced here: 683 us
  waiting for transfers between devices  348 us (50%)
  local copies, waits for them, and re-layouts  159 us (23%)
  matrix products  69.8 us (10%)
  starting transfers between devices  35.7 us (5%)
  blocking collectives  32.7 us (5%)
  other arithmetic  22.6 us (3%)
  between operations  14.8 us (2%)
    reduce_scatter x1, waiting for transfers between devices, local(): lax.psum_scatter(partials[2], 'tm', scatter_dimension=0, tiled=True)  92.4 us
    reduce_scatter x1, waiting for transfers between devices, local(): lax.psum_scatter(partials[1], 'tm', scatter_dimension=0, tiled=True)  91.8 us
    all_to_all x1, waiting for transfers between devices, local(): lax.all_to_all(slot_grad, 'tm', split_axis=0, concat_axis=0, tiled=True)  52.4 us
    unnamed x87, local copies, waits for them, and re-layouts  51.6 us
    psum x1, waiting for transfers between devices, local(): lax.psum(shares[0].astype(jnp.bfloat16), 'roll').astype(jnp.float32)  45.4 us
    ppermute x2, waiting for transfers between devices, from_behind(): return lax.ppermute(block, axis, route)  41.5 us
    all_gather x1, blocking collectives, local(): all_lists = lax.all_gather(recalled, 'tm', axis=0, tiled=True)  32.7 us
    all_to_all x1, starting transfers between devices, local(): lax.all_to_all(slot_grad, 'tm', split_axis=0, concat_axis=0, tiled=True)  23.4 us
  transfers between devices with their start and end apart: 9, of which 8 were waited for; matrix products, arithmetic and copies ran while one was open for 27% of the time, Pallas kernels for 0%

commit v1 on v0

v1 whole, which is shorter than its diff:
```python
import functools

import jax
import jax.numpy as jnp
from jax import lax
from jax.experimental import pallas as pl
from jax.experimental.pallas import tpu as pltpu
from jax.sharding import PartitionSpec as P

HEADS = 8
HEAD = 128
BAND = 4
MEM = 8
CAP = 3


masked_score = -1e30


def from_behind(block, axis, distance):
    devices = range(lax.axis_size(axis))
    route = [(i - distance, i) for i in devices if i - distance in devices]
    return lax.ppermute(block, axis, route)


def dot_last(left, right):
    return lax.dot_general(
        left, right, (((1,), (1,)), ((), ())), preferred_element_type=jnp.float32
    )


def dot_first(left, right):
    return lax.dot_general(
        left, right, (((0,), (0,)), ((), ())), preferred_element_type=jnp.float32
    )


def attend_kernel(q_ref, g_ref, ko_ref, vo_ref, kb_ref, vb_ref, ks_ref, vs_ref, bias_ref,
                  out_ref, gq_ref, gko_ref, gvo_ref, gkb_ref, gvb_ref, gks_ref, gvs_ref):
    scale = HEAD ** (-0.5)
    q = q_ref[...]
    g = g_ref[...]
    k = jnp.concatenate([ko_ref[...], kb_ref[...], ks_ref[...]], axis=0)
    v = jnp.concatenate([vo_ref[...], vb_ref[...], vs_ref[...]], axis=0)
    scores = dot_last(q, k) * scale + bias_ref[...]
    weights = jnp.exp(scores - jnp.max(scores, axis=-1, keepdims=True))
    weights = weights * (1.0 / jnp.sum(weights, axis=-1, keepdims=True))
    rounded = weights.astype(jnp.bfloat16)
    out_ref[...] = jnp.dot(rounded, v, preferred_element_type=jnp.float32).astype(jnp.bfloat16)
    grad_prob = dot_last(g, v)
    row_dot = jnp.sum(weights * grad_prob, axis=-1, keepdims=True)
    dscore = (weights * (grad_prob - row_dot)).astype(jnp.bfloat16)
    gq = jnp.dot(dscore, k, preferred_element_type=jnp.float32) * scale
    gq_ref[...] = gq.astype(jnp.bfloat16)
    gk = dot_first(dscore, q) * scale
    gv = dot_first(rounded, g)
    own = ko_ref.shape[0]
    ext = own + kb_ref.shape[0]
    gko_ref[...] = gk[:own]
    gvo_ref[...] = gv[:own]
    gkb_ref[...] = gk[own:ext].astype(jnp.bfloat16)
    gvb_ref[...] = gv[own:ext].astype(jnp.bfloat16)
    gks_ref[...] = gk[ext:].astype(jnp.bfloat16)
    gvs_ref[...] = gv[ext:].astype(jnp.bfloat16)


def attend(queries, grad_heads, key_own, value_own, before, slots, bias):
    rows, width = queries.shape
    heads = width // HEAD

    def column(count, shift=0):
        return pl.BlockSpec((count, HEAD), lambda h: (0, h + shift))

    nb, ns = before.shape[0], slots.shape[0]
    pool = rows + nb + ns
    half = jnp.bfloat16
    return pl.pallas_call(
        attend_kernel,
        grid=(heads,),
        in_specs=[
            column(rows), column(rows), column(rows), column(rows),
            column(nb), column(nb, heads), column(ns), column(ns, heads),
            pl.BlockSpec((rows, pool), lambda h: (0, 0)),
        ],
        out_specs=[
            column(rows), column(rows), column(rows), column(rows),
            column(nb), column(nb), column(ns), column(ns),
        ],
        out_shape=[
            jax.ShapeDtypeStruct((rows, width), half),
            jax.ShapeDtypeStruct((rows, width), half),
            jax.ShapeDtypeStruct((rows, width), jnp.float32),
            jax.ShapeDtypeStruct((rows, width), jnp.float32),
            jax.ShapeDtypeStruct((nb, width), half),
            jax.ShapeDtypeStruct((nb, width), half),
            jax.ShapeDtypeStruct((ns, width), half),
            jax.ShapeDtypeStruct((ns, width), half),
        ],
        compiler_params=pltpu.CompilerParams(vmem_limit_bytes=56 * 2**20),
        cost_estimate=pl.CostEstimate(
            flops=12 * rows * pool * width,
            bytes_accessed=8 * pool * width,
            transcendentals=heads * rows * pool,
        ),
        name="attend",
    )(queries, grad_heads, key_own, value_own, before, before, slots, slots, bias)


def toggled(value, mask, bit):
    k = 0
    while (1 << k) <= mask:
        if (mask >> k) & 1:
            step = 1 << k
            value = value + bit * step * (1 - 2 * ((value // step) % 2))
        k += 1
    return value


def masks_of(size):
    masks = []
    k = 0
    while (1 << k) < size:
        masks.append((1 << k) if k < 2 else (1 << k) + (1 << (k - 1)))
        k += 1
    return masks


def reduce_kernel(n_tm, n_roll, *refs):
    mats = 4
    parts, refs = refs[:mats], refs[mats:]
    outs, refs = refs[:mats], refs[mats:]
    own, refs = refs[:mats], refs[mats:]
    near, refs = refs[:mats], refs[mats:]
    far, refs = refs[:mats], refs[mats:]
    local_sem, near_send, near_recv, far_send, far_recv, share_send, share_recv = refs

    me_tm = lax.axis_index("tm")
    me_roll = lax.axis_index("roll")
    pair = ("roll", 1)
    roll_rest = [("roll", m) for m in masks_of(n_roll)[1:]]
    others = roll_rest + [("tm", m) for m in masks_of(n_tm)]
    count = len(others)
    kept = 1 << count

    def peer(direction):
        axis, mask = direction
        mine = me_tm if axis == "tm" else me_roll
        return {axis: toggled(mine, mask, 1)}

    barrier = pltpu.get_barrier_semaphore()
    for direction in [pair] + others:
        pl.semaphore_signal(
            barrier, inc=1, device_id=peer(direction), device_id_type=pl.DeviceIdType.MESH
        )
    pl.semaphore_wait(barrier, 1 + count)

    def order(m):
        shift = m % count
        return others[shift:] + others[:shift]

    def block_of(m, position, flip):
        tm, roll = me_tm, toggled(me_roll, 1, flip)
        for i, (axis, mask) in enumerate(order(m)):
            bit = (position // (1 << (count - 1 - i))) % 2
            if axis == "tm":
                tm = toggled(tm, mask, bit)
            else:
                roll = toggled(roll, mask, bit)
        return tm * n_roll + roll

    def near_copy(m, source, target):
        return pltpu.make_async_remote_copy(
            src_ref=source, dst_ref=target, send_sem=near_send.at[m], recv_sem=near_recv.at[m],
            device_id=peer(pair), device_id_type=pl.DeviceIdType.MESH,
        )

    def far_copy(m, s):
        size = kept >> (s + 1)
        return pltpu.make_async_remote_copy(
            src_ref=own[m].at[pl.ds(size, size)],
            dst_ref=far[m].at[pl.ds(size, size)],
            send_sem=far_send.at[m, s], recv_sem=far_recv.at[m, s],
            device_id=peer(order(m)[s]), device_id_type=pl.DeviceIdType.MESH,
        )

    for m in range(mats):
        @pl.loop(0, kept)
        def _(position):
            near_copy(m, parts[m].at[block_of(m, position, 1)], near[m].at[position]).start()
            pltpu.make_async_copy(
                parts[m].at[block_of(m, position, 0)], own[m].at[position], local_sem.at[m]
            ).start()

    def add(target, source, length, offset):
        @pl.loop(0, length)
        def _(i):
            total = target[i].astype(jnp.float32) + source[i + offset].astype(jnp.float32)
            target[i] = total.astype(jnp.bfloat16)

    for m in range(mats):
        whole = parts[m].at[pl.ds(0, kept)]
        pltpu.make_async_copy(whole, own[m], local_sem.at[m]).wait()
        near_copy(m, whole, near[m]).wait()
        add(own[m], near[m], kept, 0)
        far_copy(m, 0).start()

    for s in range(count):
        for m in range(mats):
            far_copy(m, s).wait()
            size = kept >> (s + 1)
            add(own[m], far[m], size, size)
            if s + 1 < count:
                far_copy(m, s + 1).start()

    for m in range(mats):
        outs[m][me_roll] = own[m][0]
    held = [0]
    index = 0
    for direction in roll_rest[::-1] + [pair]:
        def share(m, j, code):
            spot = outs[m].at[toggled_all(me_roll, code)]
            return pltpu.make_async_remote_copy(
                src_ref=spot, dst_ref=spot,
                send_sem=share_send.at[m, index + j], recv_sem=share_recv.at[m, index + j],
                device_id=peer(direction), device_id_type=pl.DeviceIdType.MESH,
            )

        for m in range(mats):
            for j, code in enumerate(held):
                share(m, j, code).start()
        for m in range(mats):
            for j, code in enumerate(held):
                share(m, j, code).wait()
        index += len(held)
        held = held + [code ^ direction[1] for code in held]


def toggled_all(value, code):
    return toggled(value, code, 1) if code else value


def reduce_all(parts, n_tm, n_roll):
    blocks = n_tm * n_roll
    kept = blocks // 2
    count = kept.bit_length() - 1
    shapes = [(p.shape[0] // blocks, p.shape[1]) for p in parts]
    half = jnp.bfloat16
    cubes = [p.reshape((blocks,) + s) for p, s in zip(parts, shapes)]
    sem = pltpu.SemaphoreType.DMA
    outs = pl.pallas_call(
        functools.partial(reduce_kernel, n_tm, n_roll),
        out_shape=[jax.ShapeDtypeStruct((n_roll,) + s, half) for s in shapes],
        in_specs=[pl.BlockSpec(memory_space=pl.ANY)] * 4,
        out_specs=[pl.BlockSpec(memory_space=pltpu.VMEM)] * 4,
        scratch_shapes=[pltpu.VMEM((kept,) + s, half) for s in shapes] * 3
        + [
            sem((4,)), sem((4,)), sem((4,)), sem((4, count)), sem((4, count)),
            sem((4, n_roll)), sem((4, n_roll)),
        ],
        compiler_params=pltpu.CompilerParams(
            collective_id=0, has_side_effects=True, vmem_limit_bytes=56 * 2**20
        ),
        name="reduce_all",
    )(*cubes)
    return [o.reshape(o.shape[0] * o.shape[1], o.shape[2]) for o in outs]


def local(inputs, cotangent, memory_lists, w_query, w_key, w_value, w_output):
    frame_count, frame_tokens, model_width = inputs.shape[1:]
    inner_width = w_query.shape[1]
    blocks = lax.axis_size("tm")
    position = lax.axis_index("tm")
    row_count = frame_count * frame_tokens
    flat_input = inputs.reshape(row_count, model_width)
    grad_flat = cotangent.reshape(row_count, model_width)
    queries = jnp.dot(flat_input, w_query, preferred_element_type=jnp.float32).astype(jnp.bfloat16)
    key_rows = jnp.dot(flat_input, w_key, preferred_element_type=jnp.float32).astype(jnp.bfloat16)
    value_rows = jnp.dot(flat_input, w_value, preferred_element_type=jnp.float32).astype(
        jnp.bfloat16
    )
    grad_heads = dot_last(grad_flat, w_output).astype(jnp.bfloat16)
    recalled = memory_lists[0]
    first_frame = position * frame_count
    last_rows = BAND * frame_tokens
    last_frames = jnp.concatenate(
        [key_rows[row_count - last_rows :], value_rows[row_count - last_rows :]], axis=-1
    )
    before = from_behind(last_frames, "tm", 1)
    all_lists = lax.all_gather(recalled, "tm", axis=0, tiled=True)
    targets = jnp.arange(blocks * frame_count, dtype=jnp.int32)
    wanted = jnp.any(recalled.reshape(-1, 1) == targets[None, :], axis=0).reshape(
        blocks, frame_count
    )
    slot_rank = jnp.cumsum(wanted.astype(jnp.int32), axis=1) - 1
    mem_ok = recalled >= 0
    slot_frame = jnp.where(
        wanted[:, None, :] & (slot_rank[:, None, :] == jnp.arange(CAP, dtype=jnp.int32)[:, None]),
        targets.reshape(blocks, 1, frame_count) + 1,
        0,
    ).sum(axis=-1).reshape(-1) - 1
    slot_ok = jnp.any(
        mem_ok[:, :, None] & (recalled[:, :, None] == slot_frame[None, None, :]), axis=1
    )
    pool_frame = first_frame + jnp.concatenate(
        [jnp.arange(frame_count, dtype=jnp.int32), jnp.arange(-BAND, 0, dtype=jnp.int32)]
    )
    ahead = (first_frame + jnp.arange(frame_count, dtype=jnp.int32))[:, None] - pool_frame[None, :]
    band_ok = (ahead >= 0) & (ahead <= BAND) & (pool_frame >= 0)[None, :]
    frame_ok = jnp.concatenate([band_ok, slot_ok], axis=1)
    bias = jnp.where(frame_ok, 0.0, masked_score).astype(jnp.float32)
    bias = jnp.repeat(jnp.repeat(bias, frame_tokens, axis=0), frame_tokens, axis=1)
    own_frames = first_frame + jnp.arange(frame_count, dtype=jnp.int32)
    requested = jnp.any(
        all_lists.reshape(blocks, frame_count * MEM, 1) == own_frames[None, None, :], axis=1
    )
    asked_rank = jnp.cumsum(requested.astype(jnp.int32), axis=1) - 1
    picker = requested[:, None, :] & (
        asked_rank[:, None, :] == jnp.arange(CAP, dtype=jnp.int32)[None, :, None]
    )
    picker = picker.astype(jnp.bfloat16)
    out_keys = jnp.einsum(
        "bcp,pz->bcz", picker, key_rows.reshape(frame_count, -1), preferred_element_type=jnp.float32
    )
    out_values = jnp.einsum(
        "bcp,pz->bcz",
        picker,
        value_rows.reshape(frame_count, -1),
        preferred_element_type=jnp.float32,
    )
    piece_shape = (blocks, CAP, frame_tokens, inner_width)
    outgoing = jnp.concatenate(
        [
            out_keys.astype(jnp.bfloat16).reshape(piece_shape),
            out_values.astype(jnp.bfloat16).reshape(piece_shape),
        ],
        axis=-1,
    )
    incoming = lax.all_to_all(outgoing, "tm", split_axis=0, concat_axis=0, tiled=True)
    slot_rows = incoming.reshape(blocks * CAP * frame_tokens, 2 * inner_width)
    (
        heads_rows, query_rows, own_keys, own_values, rim_keys, rim_values, slot_keys, slot_values
    ) = attend(queries, grad_heads, key_rows, value_rows, before, slot_rows, bias)
    rim = jnp.concatenate([rim_keys, rim_values], axis=-1)
    passed = from_behind(rim, "tm", -1)
    passed_full = jnp.pad(passed.astype(jnp.float32), ((row_count - last_rows, 0), (0, 0)))
    slot_grad = jnp.concatenate([slot_keys, slot_values], axis=-1).reshape(piece_shape[:3] + (-1,))
    returned = lax.all_to_all(slot_grad, "tm", split_axis=0, concat_axis=0, tiled=True)
    gathered_back = jnp.einsum(
        "bcp,bcz->pz", picker, returned.reshape(blocks, CAP, -1), preferred_element_type=jnp.float32
    )
    gathered_back = gathered_back.reshape(row_count, 2 * inner_width)
    grad_keys = (
        own_keys + passed_full[..., :inner_width] + gathered_back[..., :inner_width]
    ).astype(jnp.bfloat16)
    grad_values = (
        own_values + passed_full[..., inner_width:] + gathered_back[..., inner_width:]
    ).astype(jnp.bfloat16)
    grad_input = (
        dot_last(query_rows, w_query) + dot_last(grad_keys, w_key) + dot_last(grad_values, w_value)
    )
    grad_input = grad_input.astype(jnp.bfloat16).reshape(1, frame_count, frame_tokens, model_width)
    attended = jnp.dot(heads_rows, w_output, preferred_element_type=jnp.float32).astype(
        jnp.bfloat16
    )
    attended = attended.reshape(1, frame_count, frame_tokens, model_width)
    partials = (
        dot_first(flat_input, query_rows).astype(jnp.bfloat16),
        dot_first(flat_input, grad_keys).astype(jnp.bfloat16),
        dot_first(flat_input, grad_values).astype(jnp.bfloat16),
        dot_first(heads_rows, grad_flat).astype(jnp.bfloat16),
    )
    totals = [
        total.astype(jnp.float32)
        for total in reduce_all(partials, blocks, lax.axis_size("roll"))
    ]
    return (attended, grad_input, totals[0], totals[1], totals[2], totals[3])


def solution(mesh):
    return jax.shard_map(
        local,
        mesh=mesh,
        in_specs=(
            P("roll", "tm", None, None),
            P("roll", "tm", None, None),
            P("roll", "tm", None),
            P(),
            P(),
            P(),
            P(),
        ),
        out_specs=(
            P("roll", "tm", None, None),
            P("roll", "tm", None, None),
            P("tm", None),
            P("tm", None),
            P("tm", None),
            P("tm", None),
        ),
        check_vma=False,
    )
```

time: 690 us -> 402 us (0.58)
  waiting for transfers between devices: 348 us -> 99.3 us
  Pallas kernels: 0 us -> 147 us
  local copies, waits for them, and re-layouts: 159 us -> 31.3 us
  matrix products: 69.8 us -> 40.4 us
  between operations: 14.8 us -> 0.92 us
  starting transfers between devices: 35.7 us -> 25.7 us
    reduce_scatter x4 -> x0, waiting for transfers between devices: 187 us -> none  [the longest x1 92.4 us: local(): lax.psum_scatter(partials[2], 'tm', scatter_dimension=0, tiled=True)]
    pallas_call x0 -> x2, Pallas kernels: none -> 147 us  [the longest x1 129 us: reduce_all(): pl.pallas_call(functools.partial(reduce_kernel, n_tm, n_roll), out_shape=...]
    unnamed x87 -> x30, local copies, waits for them, and re-layouts: 51.6 us -> 0.64 us
    psum x1 -> x0, waiting for transfers between devices: 45.4 us -> none  [local(): lax.psum(shares[0].astype(jnp.bfloat16), 'roll').astype(jnp.float32)]
    reshape x3, local copies, waits for them, and re-layouts: 37 us -> 4.81 us  [the longest x1 3.29 us: local(): gathered_back = gathered_back.reshape(row_count, 2 * inner_width)]
    dot_general x6 -> x0, matrix products: 27.8 us -> none  [the longest x1 6.95 us: attend(): jnp.einsum('fhqk,fqhe->fkhe', rounded, grad_h, preferred_element_type=jnp...]
    all_to_all x1, waiting for transfers between devices: 52.4 us -> 31.1 us  [local(): lax.all_to_all(slot_grad, 'tm', split_axis=0, concat_axis=0, tiled=True)]
    mul x1 -> x0, local copies, waits for them, and re-layouts: 17.5 us -> none  [attend(): jnp.einsum('fhqk,fqhe->fkhe', dscore, query_h, preferred_element_type=jnp...]
  transfers between devices with their start and end apart: 9 -> 4, of which waited for: 8 -> 4; matrix products, arithmetic and copies ran while one was open for 27% -> 8% of each run, Pallas kernels for 0% -> 0%
where the time goes in v1:
time: 402 us; the launch traced here: 398 us
  Pallas kernels  147 us (37%)
  waiting for transfers between devices  99.3 us (25%)
  matrix products  40.4 us (10%)
  blocking collectives  32.7 us (8%)
  local copies, waits for them, and re-layouts  31.3 us (8%)
  starting transfers between devices  25.7 us (6%)
  other arithmetic  21.5 us (5%)
    pallas_call x1, Pallas kernels, reduce_all(): pl.pallas_call(functools.partial(reduce_kernel, n_tm, n_roll), out_shape=...  129 us
    ppermute x2, waiting for transfers between devices, from_behind(): return lax.ppermute(block, axis, route)  37 us
    all_gather x1, blocking collectives, local(): all_lists = lax.all_gather(recalled, 'tm', axis=0, tiled=True)  32.7 us
    all_to_all x1, waiting for transfers between devices, local(): lax.all_to_all(outgoing, 'tm', split_axis=0, concat_axis=0, tiled=True)  31.2 us
    all_to_all x1, waiting for transfers between devices, local(): lax.all_to_all(slot_grad, 'tm', split_axis=0, concat_axis=0, tiled=True)  31.1 us
    pallas_call x1, Pallas kernels, attend(): pl.pallas_call(attend_kernel, grid=(heads,), in_specs=[column(rows), colu...  17.3 us
    all_to_all x1, starting transfers between devices, local(): lax.all_to_all(slot_grad, 'tm', split_axis=0, concat_axis=0, tiled=True)  13.9 us
    dot_general x4, matrix products, dot_first(): lax.dot_general(left, right, (((0,), (0,)), ((), ())), preferred_element_...  13 us
  transfers between devices with their start and end apart: 4, of which 4 were waited for; matrix products, arithmetic and copies ran while one was open for 8% of the time, Pallas kernels for 0%

profile of v1, /device:TPU:0, one launch (start us, length us, event | category | flops | bytes accessed | tf_op | source)
XLA Modules:
  0.0 398.4 jit_solution(3278955426523068416)
XLA Ops:
  0.7 32.7 %all-gather = s32[1,64,8]{2,1,0:T(8,128)S(1)} all-gather(s32[1,8,8]{2,1,0:T(8,128)} %param.9), channel_id=2, replica_groups=mesh['tm'=8,'roll'=4] {'tm'}, dimensions={1}, use_global_device_ids=true | all-gather | bytes 2304 | tf_op jit(solution)/shard_map/all_gather | solution.py:289
  34.1 3.6 convolution_convert_fusion.4.vo_ref
  44.5 5.6 %all-to-all-start = ((bf16[8,3,32,2048]{3,2,1,0:T(8,128)(2,1)}), bf16[8,3,32,2048]{3,2,1,0:T(8,128)(2,1)}, u32[]{:S(2)}, u32[]{:S(2)}) async-start(bf16[8,3,32,2048]{3,2,1,0:T(8,128)(2,1)} %pad_maximum_fusion), calls=%async_computation | async-start | bytes 6291456 | tf_op jit(solution)/shard_map/all_to_all | solution.py:338
  51.0 4.8 %collective-permute-start = (bf16[128,2048]{1,0:T(8,128)(2,1)}, bf16[128,2048]{1,0:T(8,128)(2,1)}, u32[]{:S(2)}, u32[]{:S(2)}) collective-permute-start(bf16[128,2048]{1,0:T(8,128)(2,1)} %pad_maximum_fusion.2), channel_id=1, source_target_pairs={{0,4},{4,8},{8,12},{12,16},{16,20},{20,24},{24,28},{1,5},{5,9},{9,... | collective-permute-start | bytes 1572872 | tf_op jit(solution)/shard_map/ppermute | solution.py:23
  56.8 4.3 %convolution_convert_fusion.7.q_ref = bf16[256,1024]{1,0:T(8,128)(2,1)} fusion(bf16[256,2048]{1,0:T(8,128)(2,1)S(1)} %bitcast.65, bf16[2048,1024]{1,0:T(8,128)(2,1)} %param.10), kind=kOutput, calls=%fused_computation.16 | convolution fusion | flops 1074003968 | bytes 5767168 | tf_op jit(solution)/shard_map/dot_general | solution.py:276
  63.0 4.3 %convolution_convert_fusion.6.g_ref = bf16[256,1024]{1,0:T(8,128)(2,1)} fusion(bf16[256,2048]{1,0:T(8,128)(2,1)S(1)} %bitcast.81, bf16[1024,2048]{1,0:T(8,128)(2,1)} %param.13), kind=kOutput, calls=%fused_computation.15 | convolution fusion | flops 1074003968 | bytes 5767168 | tf_op jit(solution)/shard_map/dot_general | solution.py:27
  67.3 16.3 %collective-permute-done.kb_ref.vb_ref = bf16[128,2048]{1,0:T(8,128)(2,1)} collective-permute-done((bf16[128,2048]{1,0:T(8,128)(2,1)}, bf16[128,2048]{1,0:T(8,128)(2,1)}, u32[]{:S(2)}, u32[]{:S(2)}) %collective-permute-start) | collective-permute-done | bytes 524320 | tf_op jit(solution)/shard_map/ppermute | solution.py:23
  83.6 31.2 %all-to-all-done = bf16[8,3,32,2048]{3,2,1,0:T(8,128)(2,1)} async-done(((bf16[8,3,32,2048]{3,2,1,0:T(8,128)(2,1)}), bf16[8,3,32,2048]{3,2,1,0:T(8,128)(2,1)}, u32[]{:S(2)}, u32[]{:S(2)}) %all-to-all-start) | async-done | bytes 3145760 | tf_op jit(solution)/shard_map/all_to_all | solution.py:338
  114.8 17.3 %attend.1 = (bf16[256,1024]{1,0:T(8,128)(2,1)}, bf16[256,1024]{1,0:T(8,128)(2,1)}, f32[256,1024]{1,0:T(8,128)}, f32[256,1024]{1,0:T(8,128)}, bf16[128,1024]{1,0:...) custom-call(bf16[256,1024]{1,0:T(8,128)(2,1)} %convolution_convert_fusion.7.q_ref, ...), custom_call_target="tpu_custom_call" | custom-call | flops 3623878656 | bytes 9437184 | tf_op jit(solution)/shard_map/attend/pallas_call | solution.py:77
  132.1 3.9 pad_maximum_fusion.1
  136.0 13.9 %all-to-all-start.1 = ((bf16[8,3,32,2048]{3,2,1,0:T(8,128)(2,1)}), bf16[8,3,32,2048]{3,2,1,0:T(8,128)(2,1)}, u32[]{:S(2)}, u32[]{:S(2)}) async-start(bf16[8,3,32,2048]{3,2,1,0:T(8,128)(2,1)} %bitcast.75), calls=%async_computation.1 | async-start | bytes 6291456 | tf_op jit(solution)/shard_map/all_to_all | solution.py:347
  152.1 3.3 convert_bitcast_fusion.2
  155.4 3.3 convolution_convert_fusion.2
  158.7 6.4 %copy.67 = bf16[2048,1024]{1,0:T(8,128)(2,1)} copy(bf16[2048,1024]{0,1:T(8,128)(2,1)} %convert_bitcast_fusion.2) | data formatting | bytes 8388608 | tf_op jit(solution)/shard_map/convert_element_type | solution.py:367
  165.0 4.4 %convolution_convert_fusion.3 = bf16[256,2048]{1,0:T(8,128)(2,1)} fusion(bf16[256,1024]{1,0:T(8,128)(2,1)S(1)} %copy-done.7, bf16[1024,2048]{1,0:T(8,128)(2,1)} %param.13), kind=kOutput, calls=%fused_computation.12 | convolution fusion | flops 1074266112 | bytes 5767168 | tf_op jit(solution)/shard_map/dot_general | solution.py:362
  169.5 20.7 %collective-permute-done.1 = bf16[128,2048]{1,0:T(8,128)(2,1)} collective-permute-done((bf16[128,2048]{1,0:T(8,128)(2,1)}, bf16[128,2048]{1,0:T(8,128)(2,1)}, u32[]{:S(2)}, u32[]{:S(2)}) %collective-permute-start.1) | collective-permute-done | bytes 524320 | tf_op jit(solution)/shard_map/ppermute | solution.py:23
  191.4 31.1 %all-to-all-done.1 = bf16[8,3,32,2048]{3,2,1,0:T(8,128)(2,1)} async-done(((bf16[8,3,32,2048]{3,2,1,0:T(8,128)(2,1)}), bf16[8,3,32,2048]{3,2,1,0:T(8,128)(2,1)}, u32[]{:S(2)}, u32[]{:S(2)}) %all-to-all-start.1) | async-done | bytes 3145760 | tf_op jit(solution)/shard_map/all_to_all | solution.py:347
  222.5 3.6 copy.66
  226.2 2.0 convolution_bitcast_fusion
  228.2 3.3 reshape.182
  231.5 2.9 fusion.3
  236.2 3.2 convert_bitcast_fusion
  239.5 2.6 fusion.18
  242.1 3.2 convert_bitcast_fusion.1
  245.3 6.4 %copy.69 = bf16[2048,1024]{1,0:T(8,128)(2,1)} copy(bf16[2048,1024]{0,1:T(8,128)(2,1)} %convert_bitcast_fusion) | data formatting | bytes 8388608 | tf_op jit(solution)/shard_map/convert_element_type | solution.py:369
  251.7 6.4 %copy.68 = bf16[2048,1024]{1,0:T(8,128)(2,1)} copy(bf16[2048,1024]{0,1:T(8,128)(2,1)} %convert_bitcast_fusion.1) | data formatting | bytes 8388608 | tf_op jit(solution)/shard_map/convert_element_type | solution.py:368
  258.1 129.3 %reduce_all.1 = (bf16[4,64,1024]{2,1,0:T(8,128)(2,1)}, bf16[4,64,1024]{2,1,0:T(8,128)(2,1)}, bf16[4,64,1024]{2,1,0:T(8,128)(2,1)}, bf16[4,32,2048]{2,1,0:T(8,128)(2,1)}) custom-call(bf16[32,64,1024]{2,1,0:T(8,128)(2,1)} %bitcast.72, bf16[32,64,1024]{2,1,0:T(8,128)(2,1)} %bitcast.74, bf16[32,64,1024]{2,1,0:T(8,128)(2,1)} %bitcast.73, ...), custom_call_target="tpu_custom_call" | custom-call | tf_op jit(solution)/shard_map/reduce_all/pallas_call | solution.py:250
  387.5 2.3 bitcast_convert_fusion.3
  389.7 2.1 bitcast_convert_fusion.2
  391.9 2.1 bitcast_convert_fusion.1
  394.0 2.1 bitcast_convert_fusion
  396.1 2.3 fusion.1
  (75 shorter events, 16.6 us)
Async XLA Ops:
  0.6 33.4 %copy-start = (bf16[1,8,32,2048]{3,2,1,0:T(8,128)(2,1)S(1)}, bf16[1,8,32,2048]{3,2,1,0:T(8,128)(2,1)}, u32[]{:S(2)}) copy-start(bf16[1,8,32,2048]{3,2,1,0:T(8,128)(2,1)} %param.7) | copy-start | bytes 3145732
  34.1 3.6 copy-start.13
  37.7 12.4 %copy-start.5 = (bf16[256,1024]{1,0:T(8,128)(2,1)}, bf16[256,1024]{1,0:T(8,128)(2,1)S(1)}, u32[]{:S(2)}) copy-start(bf16[256,1024]{1,0:T(8,128)(2,1)S(1)} %convolution_convert_fusion.4.vo_ref) | copy-start | bytes 1572868
  39.0 11.1 %copy-start.6 = (bf16[256,1024]{1,0:T(8,128)(2,1)}, bf16[256,1024]{1,0:T(8,128)(2,1)S(1)}, u32[]{:S(2)}) copy-start(bf16[256,1024]{1,0:T(8,128)(2,1)S(1)} %convolution_convert_fusion.5.ko_ref) | copy-start | bytes 1572868
  44.5 11.3 %copy-start.11 = (s32[1,8,8]{2,1,0:T(8,128)S(1)}, s32[1,8,8]{2,1,0:T(8,128)}, u32[]{:S(2)}) copy-start(s32[1,8,8]{2,1,0:T(8,128)} %param.9) | copy-start | bytes 772
  44.5 70.3 %all-to-all-start = ((bf16[8,3,32,2048]{3,2,1,0:T(8,128)(2,1)}), bf16[8,3,32,2048]{3,2,1,0:T(8,128)(2,1)}, u32[]{:S(2)}, u32[]{:S(2)}) async-start(bf16[8,3,32,2048]{3,2,1,0:T(8,128)(2,1)} %pad_maximum_fusion), calls=%async_computation | async-start | bytes 6291456 | tf_op jit(solution)/shard_map/all_to_all | solution.py:338
  51.0 32.6 %collective-permute-start = (bf16[128,2048]{1,0:T(8,128)(2,1)}, bf16[128,2048]{1,0:T(8,128)(2,1)}, u32[]{:S(2)}, u32[]{:S(2)}) collective-permute-start(bf16[128,2048]{1,0:T(8,128)(2,1)} %pad_maximum_fusion.2), channel_id=1, source_target_pairs={{0,4},{4,8},{8,12},{12,16},{16,20},{20,24},{24,28},{1,5},{5,9},{9,... | collective-permute-start | bytes 1572872 | tf_op jit(solution)/shard_map/ppermute | solution.py:23
  56.8 6.2 %copy-start.8 = (bf16[1,8,32,2048]{3,2,1,0:T(8,128)(2,1)S(1)}, bf16[1,8,32,2048]{3,2,1,0:T(8,128)(2,1)}, u32[]{:S(2)}) copy-start(bf16[1,8,32,2048]{3,2,1,0:T(8,128)(2,1)} %param.8) | copy-start | bytes 3145732
  136.0 13.9 %copy-start.9 = (bf16[128,1024]{1,0:T(8,128)(2,1)S(1)}, bf16[128,1024]{1,0:T(8,128)(2,1)}, u32[]{:S(2)}) copy-start(bf16[128,1024]{1,0:T(8,128)(2,1)} %get-tuple-element.21) | copy-start | bytes 786436
  136.0 13.9 %copy-start.10 = (bf16[128,1024]{1,0:T(8,128)(2,1)S(1)}, bf16[128,1024]{1,0:T(8,128)(2,1)}, u32[]{:S(2)}) copy-start(bf16[128,1024]{1,0:T(8,128)(2,1)} %get-tuple-element.22) | copy-start | bytes 786436
  136.0 16.2 %copy-start.2 = (bf16[256,1024]{1,0:T(8,128)(2,1)S(1)}, bf16[256,1024]{1,0:T(8,128)(2,1)}, u32[]{:S(2)}) copy-start(bf16[256,1024]{1,0:T(8,128)(2,1)} %get-tuple-element.19) | copy-start | bytes 1572868
  136.0 86.6 %all-to-all-start.1 = ((bf16[8,3,32,2048]{3,2,1,0:T(8,128)(2,1)}), bf16[8,3,32,2048]{3,2,1,0:T(8,128)(2,1)}, u32[]{:S(2)}, u32[]{:S(2)}) async-start(bf16[8,3,32,2048]{3,2,1,0:T(8,128)(2,1)} %bitcast.75), calls=%async_computation.1 | async-start | bytes 6291456 | tf_op jit(solution)/shard_map/all_to_all | solution.py:347
  150.7 4.7 %copy-start.7 = (bf16[256,1024]{1,0:T(8,128)(2,1)S(1)}, bf16[256,1024]{1,0:T(8,128)(2,1)}, u32[]{:S(2)}) copy-start(bf16[256,1024]{1,0:T(8,128)(2,1)} %get-tuple-element.18) | copy-start | bytes 1572868
  150.7 39.4 %collective-permute-start.1 = (bf16[128,2048]{1,0:T(8,128)(2,1)}, bf16[128,2048]{1,0:T(8,128)(2,1)}, u32[]{:S(2)}, u32[]{:S(2)}) collective-permute-start(bf16[128,2048]{1,0:T(8,128)(2,1)} %pad_maximum_fusion.3), channel_id=1, source_target_pairs={{4,0},{8,4},{12,8},{16,12},{20,16},{24,20},{28,24},{5,1},{9,5},{13... | collective-permute-start | bytes 1572872 | tf_op jit(solution)/shard_map/ppermute | solution.py:23
  231.5 3.4 copy-start.12
  236.2 3.3 copy-start.14
  258.1 138.0 %copy-start.4 = (f32[256,2048]{1,0:T(8,128)S(1)}, f32[256,2048]{1,0:T(8,128)}, u32[]{:S(2)}) copy-start(f32[256,2048]{1,0:T(8,128)} %fusion.18) | copy-start | bytes 6291460
  387.4 8.7 %copy-start.1 = (bf16[2048,1024]{1,0:T(8,128)(2,1)S(1)}, bf16[2048,1024]{1,0:T(8,128)(2,1)}, u32[]{:S(2)}) copy-start(bf16[2048,1024]{1,0:T(8,128)(2,1)} %param.10) | copy-start | bytes 12582916
  387.4 8.7 %copy-start.3 = (bf16[256,1024]{1,0:T(8,128)(2,1)S(1)}, bf16[256,1024]{1,0:T(8,128)(2,1)}, u32[]{:S(2)}) copy-start(bf16[256,1024]{1,0:T(8,128)(2,1)} %get-tuple-element.19) | copy-start | bytes 1572868

commit v2 on v1

--- a/solution.py
+++ b/solution.py
@@ -239,7 +239,7 @@
     return toggled(value, code, 1) if code else value
 
 
-def reduce_all(parts, n_tm, n_roll):
+def reduce_all(parts, n_tm, n_roll, call_id):
     blocks = n_tm * n_roll
     kept = blocks // 2
     count = kept.bit_length() - 1
@@ -258,11 +258,87 @@
             sem((4, n_roll)), sem((4, n_roll)),
         ],
         compiler_params=pltpu.CompilerParams(
-            collective_id=0, has_side_effects=True, vmem_limit_bytes=56 * 2**20
+            collective_id=call_id, has_side_effects=True, vmem_limit_bytes=40 * 2**20
+        ),
+        cost_estimate=pl.CostEstimate(
+            flops=0, bytes_accessed=40 * sum(2 * p.size for p in parts), transcendentals=0
         ),
         name="reduce_all",
     )(*cubes)
     return [o.reshape(o.shape[0] * o.shape[1], o.shape[2]) for o in outs]
+
+
+def partial_kernel(x_ref, g_ref, low_ref, high_ref):
+    total = dot_first(x_ref[...], g_ref[...]).astype(jnp.bfloat16)
+    half = total.shape[1] // 2
+    low_ref[...] = total[:, :half]
+    high_ref[...] = total[:, half:]
+
+
+def partial_halves(left, right):
+    rows, depth = left.shape
+    width = right.shape[1]
+    tile = min(256, depth)
+    half = jax.ShapeDtypeStruct((depth, width // 2), jnp.bfloat16)
+    return pl.pallas_call(
+        partial_kernel,
+        grid=(depth // tile,),
+        in_specs=[
+            pl.BlockSpec((rows, tile), lambda i: (0, i)),
+            pl.BlockSpec((rows, width), lambda i: (0, 0)),
+        ],
+        out_specs=[pl.BlockSpec((tile, width // 2), lambda i: (i, 0))] * 2,
+        out_shape=[half, half],
+        compiler_params=pltpu.CompilerParams(vmem_limit_bytes=24 * 2**20),
+        cost_estimate=pl.CostEstimate(
+            flops=2 * rows * depth * width,
+            bytes_accessed=2 * (depth * width + rows * depth + rows * width),
+            transcendentals=0,
+        ),
+        name="partial_halves",
+    )(left, right)
+
+
+def lists_kernel(n_tm, lists_ref, all_ref, local_sem, send_sem, recv_sem):
+    me = lax.axis_index("tm")
+    barrier = pltpu.get_barrier_semaphore()
+    for d in range(1, n_tm):
+        pl.semaphore_signal(
+            barrier, inc=1, device_id={"tm": (me + d) % n_tm},
+            device_id_type=pl.DeviceIdType.MESH,
+        )
+    mine = pltpu.make_async_copy(lists_ref, all_ref.at[me], local_sem)
+    mine.start()
+    pl.semaphore_wait(barrier, n_tm - 1)
+    copies = [
+        pltpu.make_async_remote_copy(
+            src_ref=lists_ref, dst_ref=all_ref.at[me],
+            send_sem=send_sem.at[d], recv_sem=recv_sem.at[d],
+            device_id={"tm": (me + d) % n_tm}, device_id_type=pl.DeviceIdType.MESH,
+        )
+        for d in range(1, n_tm)
+    ]
+    for copy in copies:
+        copy.start()
+    mine.wait()
+    for copy in copies:
+        copy.wait()
+
+
+def gather_lists(lists, n_tm):
+    return pl.pallas_call(
+        functools.partial(lists_kernel, n_tm),
+        out_shape=jax.ShapeDtypeStruct((n_tm,) + lists.shape, lists.dtype),
+        in_specs=[pl.BlockSpec(memory_space=pltpu.VMEM)],
+        out_specs=pl.BlockSpec(memory_space=pltpu.VMEM),
+        scratch_shapes=[
+            pltpu.SemaphoreType.DMA,
+            pltpu.SemaphoreType.DMA((n_tm,)),
+            pltpu.SemaphoreType.DMA((n_tm,)),
+        ],
+        compiler_params=pltpu.CompilerParams(collective_id=2, has_side_effects=True),
+        name="gather_lists",
+    )(lists)
 
 
 def local(inputs, cotangent, memory_lists, w_query, w_key, w_value, w_output):
@@ -286,7 +362,7 @@
         [key_rows[row_count - last_rows :], value_rows[row_count - last_rows :]], axis=-1
     )
     before = from_behind(last_frames, "tm", 1)
-    all_lists = lax.all_gather(recalled, "tm", axis=0, tiled=True)
+    all_lists = gather_lists(recalled, blocks)
     targets = jnp.arange(blocks * frame_count, dtype=jnp.int32)
     wanted = jnp.any(recalled.reshape(-1, 1) == targets[None, :], axis=0).reshape(
         blocks, frame_count
@@ -342,9 +418,15 @@
     ) = attend(queries, grad_heads, key_rows, value_rows, before, slot_rows, bias)
     rim = jnp.concatenate([rim_keys, rim_values], axis=-1)
     passed = from_behind(rim, "tm", -1)
-    passed_full = jnp.pad(passed.astype(jnp.float32), ((row_count - last_rows, 0), (0, 0)))
     slot_grad = jnp.concatenate([slot_keys, slot_values], axis=-1).reshape(piece_shape[:3] + (-1,))
     returned = lax.all_to_all(slot_grad, "tm", split_axis=0, concat_axis=0, tiled=True)
+    rollouts = lax.axis_size("roll")
+    early = reduce_all(
+        partial_halves(flat_input, query_rows) + partial_halves(heads_rows, grad_flat),
+        blocks, rollouts, 0,
+    )
+    returned, passed, early = lax.optimization_barrier((returned, passed, early))
+    passed_full = jnp.pad(passed.astype(jnp.float32), ((row_count - last_rows, 0), (0, 0)))
     gathered_back = jnp.einsum(
         "bcp,bcz->pz", picker, returned.reshape(blocks, CAP, -1), preferred_element_type=jnp.float32
     )
@@ -363,15 +445,13 @@
         jnp.bfloat16
     )
     attended = attended.reshape(1, frame_count, frame_tokens, model_width)
-    partials = (
-        dot_first(flat_input, query_rows).astype(jnp.bfloat16),
-        dot_first(flat_input, grad_keys).astype(jnp.bfloat16),
-        dot_first(flat_input, grad_values).astype(jnp.bfloat16),
-        dot_first(heads_rows, grad_flat).astype(jnp.bfloat16),
+    late = reduce_all(
+        partial_halves(flat_input, grad_keys) + partial_halves(flat_input, grad_values),
+        blocks, rollouts, 1,
     )
     totals = [
-        total.astype(jnp.float32)
-        for total in reduce_all(partials, blocks, lax.axis_size("roll"))
+        jnp.concatenate(pieces, axis=1).astype(jnp.float32)
+        for pieces in (early[:2], late[:2], late[2:], early[2:])
     ]
     return (attended, grad_input, totals[0], totals[1], totals[2], totals[3])
 

time: 402 us -> 371 us (0.923)
  Pallas kernels: 147 us -> 235 us
  waiting for transfers between devices: 99.3 us -> 51.1 us
  blocking collectives: 32.7 us -> 0 us
  matrix products: 40.4 us -> 24.7 us
  local copies, waits for them, and re-layouts: 31.3 us -> 17.9 us
  other arithmetic: 21.5 us -> 14 us
    pallas_call x1 -> x2, Pallas kernels: 129 us -> 198 us  [reduce_all(): pl.pallas_call(functools.partial(reduce_kernel, n_tm, n_roll), out_shape=...]
    all_gather x1 -> x0, blocking collectives: 32.7 us -> none  [local(): all_lists = lax.all_gather(recalled, 'tm', axis=0, tiled=True)]
    all_to_all x1, waiting for transfers between devices: 31.1 us -> 0.01 us  [local(): lax.all_to_all(slot_grad, 'tm', split_axis=0, concat_axis=0, tiled=True)]
    pallas_call x0 -> x5, Pallas kernels: none -> 20.2 us  [the longest x4 10.4 us: partial_halves(): pl.pallas_call(partial_kernel, grid=(depth // tile,), in_specs=[pl.BlockS...]
    convert_element_type x3 -> x0, local copies, waits for them, and re-layouts: 19.1 us -> none  [the longest x1 6.39 us: local(): dot_first(flat_input, query_rows).astype(jnp.bfloat16)]
    ppermute x2, waiting for transfers between devices: 37 us -> 18.7 us  [from_behind(): return lax.ppermute(block, axis, route)]
    dot_general x4 -> x0, matrix products: 13 us -> none  [dot_first(): lax.dot_general(left, right, (((0,), (0,)), ((), ())), preferred_element_...]
    convert_element_type x4, other arithmetic: 8.64 us -> 4.35 us  [local(): jnp.concatenate(pieces, axis=1).astype(jnp.float32)]
  transfers between devices with their start and end apart: 4 -> 4, of which waited for: 4 -> 2; matrix products, arithmetic and copies ran while one was open for 8% -> 4% of each run, Pallas kernels for 0% -> 37%
where the time goes in v2:
time: 371 us; the launch traced here: 370 us
  Pallas kernels  235 us (63%)
  waiting for transfers between devices  51.1 us (14%)
  starting transfers between devices  26 us (7%)
  matrix products  24.7 us (7%)
  local copies, waits for them, and re-layouts  17.9 us (5%)
  other arithmetic  14 us (4%)
    pallas_call x2, Pallas kernels, reduce_all(): pl.pallas_call(functools.partial(reduce_kernel, n_tm, n_roll), out_shape=...  198 us
    all_to_all x1, waiting for transfers between devices, local(): lax.all_to_all(outgoing, 'tm', split_axis=0, concat_axis=0, tiled=True)  32.4 us
    ppermute x2, waiting for transfers between devices, from_behind(): return lax.ppermute(block, axis, route)  18.7 us
    pallas_call x1, Pallas kernels, attend(): pl.pallas_call(attend_kernel, grid=(heads,), in_specs=[column(rows), colu...  17.3 us
    all_to_all x1, starting transfers between devices, local(): lax.all_to_all(slot_grad, 'tm', split_axis=0, concat_axis=0, tiled=True)  14.1 us
    pallas_call x4, Pallas kernels, partial_halves(): pl.pallas_call(partial_kernel, grid=(depth // tile,), in_specs=[pl.BlockS...  10.4 us
    pallas_call x1, Pallas kernels, gather_lists(): pl.pallas_call(functools.partial(lists_kernel, n_tm), out_shape=jax.Shape...  9.81 us
    dot_general x4, matrix products, dot_last(): lax.dot_general(left, right, (((1,), (1,)), ((), ())), preferred_element_...  9.21 us
  transfers between devices with their start and end apart: 4, of which 2 were waited for; matrix products, arithmetic and copies ran while one was open for 4% of the time, Pallas kernels for 37%

profile of v2, /device:TPU:0, one launch (start us, length us, event | category | flops | bytes accessed | tf_op | source)
XLA Modules:
  0.0 369.8 jit_solution(6001649055788281060)
XLA Ops:
  0.6 9.8 %gather_lists.1 = s32[8,8,8]{2,1,0:T(8,128)} custom-call(s32[8,8]{1,0:T(8,128)} %bitcast.81), custom_call_target="tpu_custom_call" | custom-call | tf_op jit(solution)/shard_map/gather_lists/pallas_call | solution.py:329
  11.7 3.8 %convolution_convert_fusion.4.ko_ref = bf16[256,1024]{1,0:T(8,128)(2,1)S(1)} fusion(bf16[256,2048]{1,0:T(8,128)(2,1)} %bitcast.69, bf16[2048,1024]{1,0:T(8,128)(2,1)} %param.11), kind=kOutput, calls=%fused_computation.10 | convolution fusion | flops 1074003968 | bytes 5767168 | tf_op jit(solution)/shard_map/dot_general | solution.py:353
  18.2 2.1 convolution_convert_fusion.3.vo_ref
  20.3 1.3 reshape.225
  23.1 2.0 pad_maximum_fusion
  25.1 5.6 %all-to-all-start = ((bf16[8,3,32,2048]{3,2,1,0:T(8,128)(2,1)}), bf16[8,3,32,2048]{3,2,1,0:T(8,128)(2,1)}, u32[]{:S(2)}, u32[]{:S(2)}) async-start(bf16[8,3,32,2048]{3,2,1,0:T(8,128)(2,1)} %pad_maximum_fusion), calls=%async_computation | async-start | bytes 6291456 | tf_op jit(solution)/shard_map/all_to_all | solution.py:414
  30.7 4.7 %collective-permute-start = (bf16[128,2048]{1,0:T(8,128)(2,1)S(1)}, bf16[128,2048]{1,0:T(8,128)(2,1)}, u32[]{:S(2)}, u32[]{:S(2)}) collective-permute-start(bf16[128,2048]{1,0:T(8,128)(2,1)S(1)} %pad_maximum_fusion.2), channel_id=1, source_target_pairs={{0,4},{4,8},{8,12},{12,16},{16,20},{20,24},{24,28},{1,5},{5,9},{9,... | collective-permute-start | bytes 1572872 | tf_op jit(solution)/shard_map/ppermute | solution.py:23
  36.5 4.2 %convolution_convert_fusion.6.q_ref = bf16[256,1024]{1,0:T(8,128)(2,1)} fusion(bf16[256,2048]{1,0:T(8,128)(2,1)S(1)} %bitcast.71, bf16[2048,1024]{1,0:T(8,128)(2,1)} %param.10), kind=kOutput, calls=%fused_computation.12 | convolution fusion | flops 1074003968 | bytes 5767168 | tf_op jit(solution)/shard_map/dot_general | solution.py:352
  41.1 1.2 broadcast_in_dim.42
  42.3 2.7 copy.53.bias_ref
  45.0 4.3 %convolution_convert_fusion.5.g_ref = bf16[256,1024]{1,0:T(8,128)(2,1)} fusion(bf16[256,2048]{1,0:T(8,128)(2,1)S(1)} %bitcast.67, bf16[1024,2048]{1,0:T(8,128)(2,1)} %param.13), kind=kOutput, calls=%fused_computation.11 | convolution fusion | flops 1074003968 | bytes 5767168 | tf_op jit(solution)/shard_map/dot_general | solution.py:27
  49.3 18.7 %collective-permute-done.kb_ref.vb_ref = bf16[128,2048]{1,0:T(8,128)(2,1)} collective-permute-done((bf16[128,2048]{1,0:T(8,128)(2,1)S(1)}, bf16[128,2048]{1,0:T(8,128)(2,1)}, u32[]{:S(2)}, u32[]{:S(2)}) %collective-permute-start) | collective-permute-done | bytes 524320 | tf_op jit(solution)/shard_map/ppermute | solution.py:23
  68.0 32.4 %all-to-all-done = bf16[8,3,32,2048]{3,2,1,0:T(8,128)(2,1)} async-done(((bf16[8,3,32,2048]{3,2,1,0:T(8,128)(2,1)}), bf16[8,3,32,2048]{3,2,1,0:T(8,128)(2,1)}, u32[]{:S(2)}, u32[]{:S(2)}) %all-to-all-start) | async-done | bytes 3145760 | tf_op jit(solution)/shard_map/all_to_all | solution.py:414
  100.3 17.3 %attend.1 = (bf16[256,1024]{1,0:T(8,128)(2,1)}, bf16[256,1024]{1,0:T(8,128)(2,1)}, f32[256,1024]{1,0:T(8,128)}, f32[256,1024]{1,0:T(8,128)}, bf16[128,1024]{1,0:...) custom-call(bf16[256,1024]{1,0:T(8,128)(2,1)} %convolution_convert_fusion.6.q_ref, ...), custom_call_target="tpu_custom_call" | custom-call | flops 3623878656 | bytes 9437184 | tf_op jit(solution)/shard_map/attend/pallas_call | solution.py:77
  117.6 3.9 %pad_maximum_fusion.1 = bf16[768,2048]{1,0:T(8,128)(2,1)} fusion(bf16[768,1024]{1,0:T(8,128)(2,1)} %get-tuple-element.40, bf16[768,1024]{1,0:T(8,128)(2,1)} %get-tuple-element.39), kind=kLoop, calls=%fused_computation.4 | loop fusion | flops 6291456 | bytes 6291456 | tf_op jit(solution)/shard_map/concatenate | solution.py:421
  121.5 14.1 %all-to-all-start.1 = ((bf16[8,3,32,2048]{3,2,1,0:T(8,128)(2,1)}), bf16[8,3,32,2048]{3,2,1,0:T(8,128)(2,1)}, u32[]{:S(2)}, u32[]{:S(2)}) async-start(bf16[8,3,32,2048]{3,2,1,0:T(8,128)(2,1)} %bitcast.75), calls=%async_computation.1 | async-start | bytes 6291456 | tf_op jit(solution)/shard_map/all_to_all | solution.py:422
  135.7 1.6 collective-permute-start.1
  137.3 2.8 partial_halves.4
  140.2 2.0 partial_halves.5
  142.1 130.4 %reduce_all.2 = (bf16[4,64,512]{2,1,0:T(8,128)(2,1)S(1)}, bf16[4,64,512]{2,1,0:T(8,128)(2,1)S(1)}, bf16[4,32,1024]{2,1,0:T(8,128)(2,1)S(1)}, bf16[4,32,1024]{2,1,0:T(8,128)(2,1)S(1)}) custom-call(bf16[32,64,512]{2,1,0:T(8,128)(2,1)S(1)} %bitcast.55, bf16[32,64,512]{2,1,0:T(8,128)(2,1)S(1)} %bitcast.56, bf16[32,32,1024]{2,1,0:T(8,128)(2,1)S(1)} %bitcast.57, ...), custom_call_target="tpu_custom_call" | custom-call | bytes 335544320 | tf_op jit(solution)/shard_map/reduce_all/pallas_call | solution.py:250
  272.5 2.2 convolution_convert_fusion.2
  274.8 3.6 copy.54
  278.4 2.0 convolution_bitcast_fusion
  280.4 3.3 reshape.214
  283.9 1.4 copy-done.4
  285.3 2.3 fusion.3
  287.5 2.8 partial_halves.6
  290.4 1.3 fusion.18
  291.7 2.8 partial_halves.7
  294.5 1.3 fusion.19
  296.9 67.3 %reduce_all.3 = (bf16[4,64,512]{2,1,0:T(8,128)(2,1)S(1)}, bf16[4,64,512]{2,1,0:T(8,128)(2,1)S(1)}, bf16[4,64,512]{2,1,0:T(8,128)(2,1)S(1)}, bf16[4,64,512]{2,1,0:T(8,128)(2,1)S(1)}) custom-call(bf16[32,64,512]{2,1,0:T(8,128)(2,1)S(1)} %bitcast.51, bf16[32,64,512]{2,1,0:T(8,128)(2,1)S(1)} %bitcast.52, bf16[32,64,512]{2,1,0:T(8,128)(2,1)S(1)} %bitcast.53, ...), custom_call_target="tpu_custom_call" | custom-call | bytes 335544320 | tf_op jit(solution)/shard_map/reduce_all/pallas_call | solution.py:250
  367.4 2.4 fusion.1
  (73 shorter events, 11.5 us)
Async XLA Ops:
  15.5 1.1 copy-start.6
  15.5 2.0 copy-start.2
  16.0 2.3 copy-start.12
  25.1 5.6 %slice-start = ((bf16[256,1024]{1,0:T(8,128)(2,1)}), bf16[128,1024]{1,0:T(8,128)(2,1)S(1)}, s32[]{:S(2)}) async-start(bf16[256,1024]{1,0:T(8,128)(2,1)} %copy-done.6), calls=%async_computation.2 | async-start | bytes 524288 | tf_op jit(solution)/shard_map/slice | solution.py:362
  25.1 5.6 %slice-start.1 = ((bf16[256,1024]{1,0:T(8,128)(2,1)}), bf16[128,1024]{1,0:T(8,128)(2,1)S(1)}, s32[]{:S(2)}) async-start(bf16[256,1024]{1,0:T(8,128)(2,1)} %convolution_convert_fusion.3.vo_ref), calls=%async_computation.3 | async-start | bytes 524288 | tf_op jit(solution)/shard_map/slice | solution.py:362
  25.1 10.4 %copy-start.9 = (s32[1,8,8]{2,1,0:T(8,128)S(1)}, s32[1,8,8]{2,1,0:T(8,128)}, u32[]{:S(2)}) copy-start(s32[1,8,8]{2,1,0:T(8,128)} %param.9) | copy-start | bytes 772
  25.1 75.3 %all-to-all-start = ((bf16[8,3,32,2048]{3,2,1,0:T(8,128)(2,1)}), bf16[8,3,32,2048]{3,2,1,0:T(8,128)(2,1)}, u32[]{:S(2)}, u32[]{:S(2)}) async-start(bf16[8,3,32,2048]{3,2,1,0:T(8,128)(2,1)} %pad_maximum_fusion), calls=%async_computation | async-start | bytes 6291456 | tf_op jit(solution)/shard_map/all_to_all | solution.py:414
  30.7 37.3 %collective-permute-start = (bf16[128,2048]{1,0:T(8,128)(2,1)S(1)}, bf16[128,2048]{1,0:T(8,128)(2,1)}, u32[]{:S(2)}, u32[]{:S(2)}) collective-permute-start(bf16[128,2048]{1,0:T(8,128)(2,1)S(1)} %pad_maximum_fusion.2), channel_id=1, source_target_pairs={{0,4},{4,8},{8,12},{12,16},{16,20},{20,24},{24,28},{1,5},{5,9},{9,... | collective-permute-start | bytes 1572872 | tf_op jit(solution)/shard_map/ppermute | solution.py:23
  40.8 4.2 %copy-start.1 = (bf16[1,8,32,2048]{3,2,1,0:T(8,128)(2,1)S(1)}, bf16[1,8,32,2048]{3,2,1,0:T(8,128)(2,1)}, u32[]{:S(2)}) copy-start(bf16[1,8,32,2048]{3,2,1,0:T(8,128)(2,1)} %param.8) | copy-start | bytes 3145732
  121.5 14.1 %copy-start.7 = (bf16[128,1024]{1,0:T(8,128)(2,1)S(1)}, bf16[128,1024]{1,0:T(8,128)(2,1)}, u32[]{:S(2)}) copy-start(bf16[128,1024]{1,0:T(8,128)(2,1)} %get-tuple-element.41) | copy-start | bytes 786436
  121.5 14.1 %copy-start.8 = (bf16[128,1024]{1,0:T(8,128)(2,1)S(1)}, bf16[128,1024]{1,0:T(8,128)(2,1)}, u32[]{:S(2)}) copy-start(bf16[128,1024]{1,0:T(8,128)(2,1)} %get-tuple-element.42) | copy-start | bytes 786436
  121.5 15.8 %copy-start = (bf16[256,1024]{1,0:T(8,128)(2,1)S(1)}, bf16[256,1024]{1,0:T(8,128)(2,1)}, u32[]{:S(2)}) copy-start(bf16[256,1024]{1,0:T(8,128)(2,1)} %get-tuple-element.37.g_ref) | copy-start | bytes 1572868
  121.5 153.2 %all-to-all-start.1 = ((bf16[8,3,32,2048]{3,2,1,0:T(8,128)(2,1)}), bf16[8,3,32,2048]{3,2,1,0:T(8,128)(2,1)}, u32[]{:S(2)}, u32[]{:S(2)}) async-start(bf16[8,3,32,2048]{3,2,1,0:T(8,128)(2,1)} %bitcast.75), calls=%async_computation.1 | async-start | bytes 6291456 | tf_op jit(solution)/shard_map/all_to_all | solution.py:422
  135.6 4.5 %copy-start.3 = (bf16[256,1024]{1,0:T(8,128)(2,1)S(1)}, bf16[256,1024]{1,0:T(8,128)(2,1)}, u32[]{:S(2)}) copy-start(bf16[256,1024]{1,0:T(8,128)(2,1)} %get-tuple-element.36.x_ref) | copy-start | bytes 1572868
  135.7 139.1 %collective-permute-start.1 = (bf16[128,2048]{1,0:T(8,128)(2,1)S(1)}, bf16[128,2048]{1,0:T(8,128)(2,1)S(1)}, u32[]{:S(2)}, u32[]{:S(2)}) collective-permute-start(bf16[128,2048]{1,0:T(8,128)(2,1)S(1)} %pad_maximum_fusion.3), channel_id=1, source_target_pairs={{4,0},{8,4},{12,8},{16,12},{20,16},{24,20},{28,24},{5,1},{9,5},{13... | collective-permute-start | bytes 1572872 | tf_op jit(solution)/shard_map/ppermute | solution.py:23
  142.1 130.4 %copy-start.10 = (bf16[1024,2048]{1,0:T(8,128)(2,1)S(1)}, bf16[1024,2048]{1,0:T(8,128)(2,1)}, u32[]{:S(2)}) copy-start(bf16[1024,2048]{1,0:T(8,128)(2,1)} %param.13) | copy-start | bytes 12582916
  283.7 1.6 copy-start.4
  285.3 5.1 %copy-start.11 = (bf16[2048,1024]{1,0:T(8,128)(2,1)S(1)}, bf16[2048,1024]{1,0:T(8,128)(2,1)}, u32[]{:S(2)}) copy-start(bf16[2048,1024]{1,0:T(8,128)(2,1)} %param.11) | copy-start | bytes 12582916
  290.4 4.1 %copy-start.13 = (bf16[2048,1024]{1,0:T(8,128)(2,1)S(1)}, bf16[2048,1024]{1,0:T(8,128)(2,1)}, u32[]{:S(2)}) copy-start(bf16[2048,1024]{1,0:T(8,128)(2,1)} %param.12) | copy-start | bytes 12582916
  364.1 3.3 copy-start.5

commit v3 on v2

--- a/solution.py
+++ b/solution.py
@@ -125,14 +125,13 @@
     return masks
 
 
-def reduce_kernel(n_tm, n_roll, *refs):
+def reduce_kernel(n_tm, n_roll, across_first, *refs):
     mats = 4
     parts, refs = refs[:mats], refs[mats:]
     outs, refs = refs[:mats], refs[mats:]
     own, refs = refs[:mats], refs[mats:]
-    near, refs = refs[:mats], refs[mats:]
     far, refs = refs[:mats], refs[mats:]
-    local_sem, near_send, near_recv, far_send, far_recv, share_send, share_recv = refs
+    local_sem, far_send, far_recv, share_send, share_recv = refs
 
     me_tm = lax.axis_index("tm")
     me_roll = lax.axis_index("roll")
@@ -155,24 +154,20 @@
     pl.semaphore_wait(barrier, 1 + count)
 
     def order(m):
+        if across_first:
+            return others if m % 2 == 0 else others[1::-1] + others[:1:-1]
         shift = m % count
         return others[shift:] + others[:shift]
 
-    def block_of(m, position, flip):
-        tm, roll = me_tm, toggled(me_roll, 1, flip)
+    def block_of(m, position):
+        tm, roll = me_tm, me_roll
         for i, (axis, mask) in enumerate(order(m)):
             bit = (position // (1 << (count - 1 - i))) % 2
             if axis == "tm":
                 tm = toggled(tm, mask, bit)
             else:
                 roll = toggled(roll, mask, bit)
-        return tm * n_roll + roll
-
-    def near_copy(m, source, target):
-        return pltpu.make_async_remote_copy(
-            src_ref=source, dst_ref=target, send_sem=near_send.at[m], recv_sem=near_recv.at[m],
-            device_id=peer(pair), device_id_type=pl.DeviceIdType.MESH,
-        )
+        return tm * (n_roll // 2) + roll // 2
 
     def far_copy(m, s):
         size = kept >> (s + 1)
@@ -186,9 +181,8 @@
     for m in range(mats):
         @pl.loop(0, kept)
         def _(position):
-            near_copy(m, parts[m].at[block_of(m, position, 1)], near[m].at[position]).start()
             pltpu.make_async_copy(
-                parts[m].at[block_of(m, position, 0)], own[m].at[position], local_sem.at[m]
+                parts[m].at[block_of(m, position)], own[m].at[position], local_sem.at[m]
             ).start()
 
     def add(target, source, length, offset):
@@ -198,10 +192,7 @@
             target[i] = total.astype(jnp.bfloat16)
 
     for m in range(mats):
-        whole = parts[m].at[pl.ds(0, kept)]
-        pltpu.make_async_copy(whole, own[m], local_sem.at[m]).wait()
-        near_copy(m, whole, near[m]).wait()
-        add(own[m], near[m], kept, 0)
+        pltpu.make_async_copy(parts[m], own[m], local_sem.at[m]).wait()
         far_copy(m, 0).start()
 
     for s in range(count):
@@ -240,21 +231,21 @@
 
 
 def reduce_all(parts, n_tm, n_roll, call_id):
-    blocks = n_tm * n_roll
-    kept = blocks // 2
+    kept = n_tm * n_roll // 2
+    blocks = kept
     count = kept.bit_length() - 1
     shapes = [(p.shape[0] // blocks, p.shape[1]) for p in parts]
     half = jnp.bfloat16
     cubes = [p.reshape((blocks,) + s) for p, s in zip(parts, shapes)]
     sem = pltpu.SemaphoreType.DMA
     outs = pl.pallas_call(
-        functools.partial(reduce_kernel, n_tm, n_roll),
+        functools.partial(reduce_kernel, n_tm, n_roll, call_id == 0),
         out_shape=[jax.ShapeDtypeStruct((n_roll,) + s, half) for s in shapes],
         in_specs=[pl.BlockSpec(memory_space=pl.ANY)] * 4,
         out_specs=[pl.BlockSpec(memory_space=pltpu.VMEM)] * 4,
-        scratch_shapes=[pltpu.VMEM((kept,) + s, half) for s in shapes] * 3
+        scratch_shapes=[pltpu.VMEM((kept,) + s, half) for s in shapes] * 2
         + [
-            sem((4,)), sem((4,)), sem((4,)), sem((4, count)), sem((4, count)),
+            sem((4,)), sem((4, count)), sem((4, count)),
             sem((4, n_roll)), sem((4, n_roll)),
         ],
         compiler_params=pltpu.CompilerParams(
@@ -265,38 +256,57 @@
         ),
         name="reduce_all",
     )(*cubes)
-    return [o.reshape(o.shape[0] * o.shape[1], o.shape[2]) for o in outs]
-
-
-def partial_kernel(x_ref, g_ref, low_ref, high_ref):
-    total = dot_first(x_ref[...], g_ref[...]).astype(jnp.bfloat16)
+    return outs
+
+
+def assembled(low, high):
+    n_roll, rows, width = low.shape
+    both = jnp.stack([low, high], axis=2).reshape(n_roll // 2, 2, rows, 2 * width)
+    return both.transpose(0, 2, 1, 3).reshape(n_roll // 2 * rows, 4 * width).astype(jnp.float32)
+
+
+def from_pair(block):
+    return lax.ppermute(block, "roll", [(i, i ^ 1) for i in range(lax.axis_size("roll"))])
+
+
+def column_halves(block):
+    half = block.shape[1] // 2
+    core = lax.axis_index("roll") % 2
+    return (
+        lax.dynamic_slice_in_dim(block, core * half, half, 1),
+        lax.dynamic_slice_in_dim(block, (1 - core) * half, half, 1),
+    )
+
+
+def partial_kernel(x_ref, y_ref, g_ref, h_ref, low_ref, high_ref):
+    total = dot_first(x_ref[...], g_ref[...]) + dot_first(y_ref[...], h_ref[...])
+    total = total.astype(jnp.bfloat16)
     half = total.shape[1] // 2
     low_ref[...] = total[:, :half]
     high_ref[...] = total[:, half:]
 
 
-def partial_halves(left, right):
+def partial_halves(left, left_pair, right, right_pair):
     rows, depth = left.shape
     width = right.shape[1]
     tile = min(256, depth)
     half = jax.ShapeDtypeStruct((depth, width // 2), jnp.bfloat16)
+    left_spec = pl.BlockSpec((rows, tile), lambda i: (0, i))
+    right_spec = pl.BlockSpec((rows, width), lambda i: (0, 0))
     return pl.pallas_call(
         partial_kernel,
         grid=(depth // tile,),
-        in_specs=[
-            pl.BlockSpec((rows, tile), lambda i: (0, i)),
-            pl.BlockSpec((rows, width), lambda i: (0, 0)),
-        ],
+        in_specs=[left_spec, left_spec, right_spec, right_spec],
         out_specs=[pl.BlockSpec((tile, width // 2), lambda i: (i, 0))] * 2,
         out_shape=[half, half],
         compiler_params=pltpu.CompilerParams(vmem_limit_bytes=24 * 2**20),
         cost_estimate=pl.CostEstimate(
-            flops=2 * rows * depth * width,
-            bytes_accessed=2 * (depth * width + rows * depth + rows * width),
+            flops=4 * rows * depth * width,
+            bytes_accessed=2 * (depth * width + 2 * rows * depth + 2 * rows * width),
             transcendentals=0,
         ),
         name="partial_halves",
-    )(left, right)
+    )(left, left_pair, right, right_pair)
 
 
 def lists_kernel(n_tm, lists_ref, all_ref, local_sem, send_sem, recv_sem):
@@ -355,6 +365,9 @@
         jnp.bfloat16
     )
     grad_heads = dot_last(grad_flat, w_output).astype(jnp.bfloat16)
+    input_pair = from_pair(flat_input)
+    grad_keep, grad_give = column_halves(grad_flat)
+    grad_pair = from_pair(grad_give)
     recalled = memory_lists[0]
     first_frame = position * frame_count
     last_rows = BAND * frame_tokens
@@ -412,6 +425,9 @@
         axis=-1,
     )
     incoming = lax.all_to_all(outgoing, "tm", split_axis=0, concat_axis=0, tiled=True)
+    incoming, before, input_pair, grad_pair = lax.optimization_barrier(
+        (incoming, before, input_pair, grad_pair)
+    )
     slot_rows = incoming.reshape(blocks * CAP * frame_tokens, 2 * inner_width)
     (
         heads_rows, query_rows, own_keys, own_values, rim_keys, rim_values, slot_keys, slot_values
@@ -421,8 +437,10 @@
     slot_grad = jnp.concatenate([slot_keys, slot_values], axis=-1).reshape(piece_shape[:3] + (-1,))
     returned = lax.all_to_all(slot_grad, "tm", split_axis=0, concat_axis=0, tiled=True)
     rollouts = lax.axis_size("roll")
+    query_keep, query_give = column_halves(query_rows)
     early = reduce_all(
-        partial_halves(flat_input, query_rows) + partial_halves(heads_rows, grad_flat),
+        partial_halves(flat_input, input_pair, query_keep, from_pair(query_give))
+        + partial_halves(heads_rows, from_pair(heads_rows), grad_keep, grad_pair),
         blocks, rollouts, 0,
     )
     returned, passed, early = lax.optimization_barrier((returned, passed, early))
@@ -445,12 +463,15 @@
         jnp.bfloat16
     )
     attended = attended.reshape(1, frame_count, frame_tokens, model_width)
+    key_keep, key_give = column_halves(grad_keys)
+    value_keep, value_give = column_halves(grad_values)
     late = reduce_all(
-        partial_halves(flat_input, grad_keys) + partial_halves(flat_input, grad_values),
+        partial_halves(flat_input, input_pair, key_keep, from_pair(key_give))
+        + partial_halves(flat_input, input_pair, value_keep, from_pair(value_give)),
         blocks, rollouts, 1,
     )
     totals = [
-        jnp.concatenate(pieces, axis=1).astype(jnp.float32)
+        assembled(*pieces)
         for pieces in (early[:2], late[:2], late[2:], early[2:])
     ]
     return (attended, grad_input, totals[0], totals[1], totals[2], totals[3])

time: 371 us -> 356 us (0.960)
  Pallas kernels: 235 us -> 197 us
  local copies, waits for them, and re-layouts: 17.9 us -> 40.6 us
  waiting for transfers between devices: 51.1 us -> 46.5 us
  matrix products: 24.7 us -> 28.9 us
    pallas_call x6, Pallas kernels: 208 us -> 170 us  [the longest x2 158 us: reduce_all(): pl.pallas_call(functools.partial(reduce_kernel, n_tm, n_roll, call_id ==...]
    convert_element_type x0 -> x9, local copies, waits for them, and re-layouts: none -> 11.4 us  [assembled(): both.transpose(0, 2, 1, 3).reshape(n_roll // 2 * rows, 4 * width)]
    unnamed x28 -> x32, local copies, waits for them, and re-layouts: 2.21 us -> 7.93 us
    dynamic_slice x0 -> x4, local copies, waits for them, and re-layouts: none -> 4.63 us  [the longest x3 2.57 us: column_halves(): lax.dynamic_slice_in_dim(block, (1 - core) * half, half, 1)]
    ppermute x2, waiting for transfers between devices: 18.7 us -> 14.2 us  [from_behind(): return lax.ppermute(block, axis, route)]
    dot_general x4, matrix products: 9.21 us -> 13.4 us  [dot_last(): lax.dot_general(left, right, (((1,), (1,)), ((), ())), preferred_element_...]
  transfers between devices with their start and end apart: 4 -> 10, of which waited for: 2 -> 2; matrix products, arithmetic and copies ran while one was open for 4% -> 13% of each run, Pallas kernels for 37% -> 29%
where the time goes in v3:
time: 356 us; the launch traced here: 355 us
  Pallas kernels  197 us (55%)
  waiting for transfers between devices  46.5 us (13%)
  local copies, waits for them, and re-layouts  40.6 us (11%)
  matrix products  28.9 us (8%)
  starting transfers between devices  27.3 us (8%)
  other arithmetic  13 us (4%)
    pallas_call x2, Pallas kernels, reduce_all(): pl.pallas_call(functools.partial(reduce_kernel, n_tm, n_roll, call_id ==...  158 us
    all_to_all x1, waiting for transfers between devices, local(): lax.all_to_all(outgoing, 'tm', split_axis=0, concat_axis=0, tiled=True)  32.2 us
    pallas_call x1, Pallas kernels, attend(): pl.pallas_call(attend_kernel, grid=(heads,), in_specs=[column(rows), colu...  17.3 us
    all_to_all x1, starting transfers between devices, local(): lax.all_to_all(slot_grad, 'tm', split_axis=0, concat_axis=0, tiled=True)  14.3 us
    ppermute x2, waiting for transfers between devices, from_behind(): return lax.ppermute(block, axis, route)  14.2 us
    dot_general x4, matrix products, dot_last(): lax.dot_general(left, right, (((1,), (1,)), ((), ())), preferred_element_...  13.4 us
    pallas_call x4, Pallas kernels, partial_halves(): pl.pallas_call(partial_kernel, grid=(depth // tile,), in_specs=[left_spec...  11.8 us
    convert_element_type x9, local copies, waits for them, and re-layouts, assembled(): both.transpose(0, 2, 1, 3).reshape(n_roll // 2 * rows, 4 * width)  11.4 us
  transfers between devices with their start and end apart: 10, of which 2 were waited for; matrix products, arithmetic and copies ran while one was open for 13% of the time, Pallas kernels for 29%

profile of v3, /device:TPU:0, one launch (start us, length us, event | category | flops | bytes accessed | tf_op | source)
XLA Modules:
  0.0 354.7 jit_solution(8568825452738169029)
XLA Ops:
  0.6 9.8 %gather_lists.1 = s32[8,8,8]{2,1,0:T(8,128)} custom-call(s32[8,8]{1,0:T(8,128)} %bitcast.115), custom_call_target="tpu_custom_call" | custom-call | tf_op jit(solution)/shard_map/gather_lists/pallas_call | solution.py:339
  11.7 3.8 %convolution_convert_fusion.4.ko_ref = bf16[256,1024]{1,0:T(8,128)(2,1)S(1)} fusion(bf16[256,2048]{1,0:T(8,128)(2,1)} %bitcast.89, bf16[2048,1024]{1,0:T(8,128)(2,1)} %param.11), kind=kOutput, calls=%fused_computation.10 | convolution fusion | flops 1074003968 | bytes 5767168 | tf_op jit(solution)/shard_map/dot_general | solution.py:363
  18.3 2.1 convolution_convert_fusion.3.vo_ref
  23.1 2.0 pad_maximum_fusion
  25.1 5.5 %all-to-all-start = ((bf16[8,3,32,2048]{3,2,1,0:T(8,128)(2,1)}), bf16[8,3,32,2048]{3,2,1,0:T(8,128)(2,1)}, u32[]{:S(2)}, u32[]{:S(2)}) async-start(bf16[8,3,32,2048]{3,2,1,0:T(8,128)(2,1)} %pad_maximum_fusion), calls=%async_computation | async-start | bytes 6291456 | tf_op jit(solution)/shard_map/all_to_all | solution.py:427
  30.7 2.1 constant_dynamic-slice_fusion.4
  35.1 4.6 %collective-permute-start = (bf16[128,2048]{1,0:T(8,128)(2,1)}, bf16[128,2048]{1,0:T(8,128)(2,1)}, u32[]{:S(2)}, u32[]{:S(2)}) collective-permute-start(bf16[128,2048]{1,0:T(8,128)(2,1)} %pad_maximum_fusion.2), channel_id=1, source_target_pairs={{0,4},{4,8},{8,12},{12,16},{16,20},{20,24},{24,28},{1,5},{5,9},{9,... | collective-permute-start | bytes 1572872 | tf_op jit(solution)/shard_map/ppermute | solution.py:23
  40.8 4.2 %convolution_convert_fusion.6.q_ref = bf16[256,1024]{1,0:T(8,128)(2,1)} fusion(bf16[256,2048]{1,0:T(8,128)(2,1)S(1)} %bitcast.92, bf16[2048,1024]{1,0:T(8,128)(2,1)} %param.10), kind=kOutput, calls=%fused_computation.12 | convolution fusion | flops 1074003968 | bytes 5767168 | tf_op jit(solution)/shard_map/dot_general | solution.py:362
  46.6 2.6 copy.73.bias_ref
  49.2 4.6 %convolution_convert_fusion.5.g_ref = bf16[256,1024]{1,0:T(8,128)(2,1)} fusion(bf16[256,2048]{1,0:T(8,128)(2,1)} %bitcast.114, bf16[1024,2048]{1,0:T(8,128)(2,1)} %param.13), kind=kOutput, calls=%fused_computation.11 | convolution fusion | flops 1074003968 | bytes 5767168 | tf_op jit(solution)/shard_map/dot_general | solution.py:27
  53.8 14.2 %collective-permute-done.kb_ref.vb_ref = bf16[128,2048]{1,0:T(8,128)(2,1)} collective-permute-done((bf16[128,2048]{1,0:T(8,128)(2,1)}, bf16[128,2048]{1,0:T(8,128)(2,1)}, u32[]{:S(2)}, u32[]{:S(2)}) %collective-permute-start) | collective-permute-done | bytes 524320 | tf_op jit(solution)/shard_map/ppermute | solution.py:23
  68.0 32.2 %all-to-all-done = bf16[8,3,32,2048]{3,2,1,0:T(8,128)(2,1)} async-done(((bf16[8,3,32,2048]{3,2,1,0:T(8,128)(2,1)}), bf16[8,3,32,2048]{3,2,1,0:T(8,128)(2,1)}, u32[]{:S(2)}, u32[]{:S(2)}) %all-to-all-start) | async-done | bytes 3145760 | tf_op jit(solution)/shard_map/all_to_all | solution.py:427
  100.3 17.3 %attend.1 = (bf16[256,1024]{1,0:T(8,128)(2,1)}, bf16[256,1024]{1,0:T(8,128)(2,1)}, f32[256,1024]{1,0:T(8,128)}, f32[256,1024]{1,0:T(8,128)}, bf16[128,1024]{1,0:...) custom-call(bf16[256,1024]{1,0:T(8,128)(2,1)} %convolution_convert_fusion.6.q_ref, ...), custom_call_target="tpu_custom_call" | custom-call | flops 3623878656 | bytes 9437184 | tf_op jit(solution)/shard_map/attend/pallas_call | solution.py:77
  117.6 3.9 %pad_maximum_fusion.1 = bf16[768,2048]{1,0:T(8,128)(2,1)} fusion(bf16[768,1024]{1,0:T(8,128)(2,1)} %get-tuple-element.46, bf16[768,1024]{1,0:T(8,128)(2,1)} %get-tuple-element.45), kind=kLoop, calls=%fused_computation.4 | loop fusion | flops 6291456 | bytes 6291456 | tf_op jit(solution)/shard_map/concatenate | solution.py:437
  121.5 14.3 %all-to-all-start.1 = ((bf16[8,3,32,2048]{3,2,1,0:T(8,128)(2,1)}), bf16[8,3,32,2048]{3,2,1,0:T(8,128)(2,1)}, u32[]{:S(2)}, u32[]{:S(2)}) async-start(bf16[8,3,32,2048]{3,2,1,0:T(8,128)(2,1)} %bitcast.96), calls=%async_computation.1 | async-start | bytes 6291456 | tf_op jit(solution)/shard_map/all_to_all | solution.py:438
  137.5 5.3 %fusion.17 = f32[256,2048]{1,0:T(8,128)} fusion(bf16[256,1024]{1,0:T(8,128)(2,1)} %get-tuple-element.43, bf16[2048,1024]{1,0:T(8,128)(2,1)} %param.10), kind=kOutput, calls=%fused_computation.63 | convolution fusion | flops 1073741824 | bytes 6815744 | tf_op jit(solution)/shard_map/dot_general | solution.py:27
  144.1 2.2 convolution_convert_fusion.2
  146.4 3.0 partial_halves.4
  149.3 2.0 partial_halves.5
  151.4 93.3 %reduce_all.2 = (bf16[4,128,256]{2,1,0:T(8,128)(2,1)S(1)}, bf16[4,128,256]{2,1,0:T(8,128)(2,1)S(1)}, bf16[4,64,512]{2,1,0:T(8,128)(2,1)S(1)}, bf16[4,64,512]{2,1,0:T(8,128)(2,1)S(1)}) custom-call(bf16[16,128,256]{2,1,0:T(8,128)(2,1)S(1)} %bitcast.73, bf16[16,128,256]{2,1,0:T(8,128)(2,1)S(1)} %bitcast.74, bf16[16,64,512]{2,1,0:T(8,128)(2,1)S(1)} %bitcast.77, ...), custom_call_target="tpu_custom_call" | custom-call | bytes 167772160 | tf_op jit(solution)/shard_map/reduce_all/pallas_call | solution.py:241
  244.8 3.6 %copy.74 = bf16[8,3,32,2048]{3,0,2,1:T(8,128)(2,1)S(1)} copy(bf16[8,3,32,2048]{3,2,1,0:T(8,128)(2,1)} %all-to-all-done.1) | data formatting | bytes 6291456 | tf_op jit(solution)/shard_map/optimization_barrier | solution.py:446
  248.4 2.0 convolution_bitcast_fusion
  250.4 3.3 reshape.210
  255.4 2.3 fusion.1
  261.8 2.3 fusion
  266.8 2.0 copy.82
  271.2 2.6 copy.75
  273.8 2.2 copy.76
  276.1 2.4 copy.85
  278.5 3.9 %partial_halves.7 = (bf16[2048,256]{1,0:T(8,128)(2,1)S(1)}, bf16[2048,256]{1,0:T(8,128)(2,1)S(1)}) custom-call(bf16[256,2048]{1,0:T(8,128)(2,1)S(1)} %bitcast.94, bf16[256,2048]{1,0:T(8,128)(2,1)S(1)} %copy-done.2, bf16[256,512]{1,0:T(8,128)(2,1)S(1)} %get-tuple-element.81.g_ref, bf16[256,512]{1,0:T(8,128)(2,1)} %collective-permute-done.7.h_ref), custom_call_target="tpu_custom_call" | custom-call | flops 1073741824 | bytes 4718592 | tf_op jit(solution)/shard_map/partial_halves/pallas_call | solution.py:296
  282.4 3.0 partial_halves.6
  285.3 65.0 %reduce_all.3 = (bf16[4,128,256]{2,1,0:T(8,128)(2,1)S(1)}, bf16[4,128,256]{2,1,0:T(8,128)(2,1)S(1)}, bf16[4,128,256]{2,1,0:T(8,128)(2,1)S(1)}, bf16[4,128,256]{2,1,0:T(8,128)(2,1)S(1)}) custom-call(bf16[16,128,256]{2,1,0:T(8,128)(2,1)S(1)} %bitcast.79, bf16[16,128,256]{2,1,0:T(8,128)(2,1)S(1)} %bitcast.80, bf16[16,128,256]{2,1,0:T(8,128)(2,1)S(1)} %bitcast.75, ...), custom_call_target="tpu_custom_call" | custom-call | bytes 167772160 | tf_op jit(solution)/shard_map/reduce_all/pallas_call | solution.py:241
  (101 shorter events, 29.9 us)
Async XLA Ops:
  15.5 1.1 copy-start.7
  15.5 2.0 copy-start
  16.0 2.3 copy-start.12
  25.1 75.1 %all-to-all-start = ((bf16[8,3,32,2048]{3,2,1,0:T(8,128)(2,1)}), bf16[8,3,32,2048]{3,2,1,0:T(8,128)(2,1)}, u32[]{:S(2)}, u32[]{:S(2)}) async-start(bf16[8,3,32,2048]{3,2,1,0:T(8,128)(2,1)} %pad_maximum_fusion), calls=%async_computation | async-start | bytes 6291456 | tf_op jit(solution)/shard_map/all_to_all | solution.py:427
  30.6 3.6 %slice-start = ((bf16[256,1024]{1,0:T(8,128)(2,1)}), bf16[128,1024]{1,0:T(8,128)(2,1)S(1)}, s32[]{:S(2)}) async-start(bf16[256,1024]{1,0:T(8,128)(2,1)} %copy-done.7), calls=%async_computation.2 | async-start | bytes 524288 | tf_op jit(solution)/shard_map/slice | solution.py:375
  30.6 9.1 %copy-start.10 = (s32[1,8,8]{2,1,0:T(8,128)S(1)}, s32[1,8,8]{2,1,0:T(8,128)}, u32[]{:S(2)}) copy-start(s32[1,8,8]{2,1,0:T(8,128)} %param.9) | copy-start | bytes 772
  30.6 37.4 %collective-permute-start.1 = (bf16[256,2048]{1,0:T(8,128)(2,1)S(1)}, bf16[256,2048]{1,0:T(8,128)(2,1)S(1)}, u32[]{:S(2)}, u32[]{:S(2)}) collective-permute-start(bf16[256,2048]{1,0:T(8,128)(2,1)S(1)} %bitcast.91), channel_id=1, source_target_pairs={{0,1},{1,0},{2,3},{3,2},{4,5},{5,4},{6,7},{7,6},{8,9},{9,8},{10,11... | collective-permute-start | bytes 3145736 | tf_op jit(solution)/shard_map/ppermute | solution.py:269
  32.8 21.0 %collective-permute-start.2 = (bf16[256,1024]{1,0:T(8,128)(2,1)}, bf16[256,1024]{1,0:T(8,128)(2,1)S(1)}, u32[]{:S(2)}, u32[]{:S(2)}) collective-permute-start(bf16[256,1024]{1,0:T(8,128)(2,1)} %get-tuple-element.79), channel_id=1, source_target_pairs={{0,1},{1,0},{2,3},{3,2},{4,5},{5,4},{6,7},{7,6},{8,9},{9,8},{10,11... | collective-permute-start | bytes 1572872 | tf_op jit(solution)/shard_map/ppermute | solution.py:269
  35.1 33.0 %collective-permute-start = (bf16[128,2048]{1,0:T(8,128)(2,1)}, bf16[128,2048]{1,0:T(8,128)(2,1)}, u32[]{:S(2)}, u32[]{:S(2)}) collective-permute-start(bf16[128,2048]{1,0:T(8,128)(2,1)} %pad_maximum_fusion.2), channel_id=1, source_target_pairs={{0,4},{4,8},{8,12},{12,16},{16,20},{20,24},{24,28},{1,5},{5,9},{9,... | collective-permute-start | bytes 1572872 | tf_op jit(solution)/shard_map/ppermute | solution.py:23
  68.0 78.3 %copy-start.1 = (bf16[256,2048]{1,0:T(8,128)(2,1)}, bf16[256,2048]{1,0:T(8,128)(2,1)S(1)}, u32[]{:S(2)}) copy-start(bf16[256,2048]{1,0:T(8,128)(2,1)S(1)} %collective-permute-done.1.y_ref) | copy-start | bytes 3145732
  121.5 123.3 %all-to-all-start.1 = ((bf16[8,3,32,2048]{3,2,1,0:T(8,128)(2,1)}), bf16[8,3,32,2048]{3,2,1,0:T(8,128)(2,1)}, u32[]{:S(2)}, u32[]{:S(2)}) async-start(bf16[8,3,32,2048]{3,2,1,0:T(8,128)(2,1)} %bitcast.96), calls=%async_computation.1 | async-start | bytes 6291456 | tf_op jit(solution)/shard_map/all_to_all | solution.py:438
  135.8 13.5 %collective-permute-start.5 = (bf16[256,1024]{1,0:T(8,128)(2,1)}, bf16[256,1024]{1,0:T(8,128)(2,1)S(1)}, u32[]{:S(2)}, u32[]{:S(2)}) collective-permute-start(bf16[256,1024]{1,0:T(8,128)(2,1)} %get-tuple-element.42.x_ref), channel_id=1, source_target_pairs={{0,1},{1,0},{2,3},{3,2},{4,5},{5,4},{6,7},{7,6},{8,9},{9,8},{10,11... | collective-permute-start | bytes 1572872 | tf_op jit(solution)/shard_map/ppermute | solution.py:269
  136.9 5.9 %copy-start.8 = (bf16[128,1024]{1,0:T(8,128)(2,1)S(1)}, bf16[128,1024]{1,0:T(8,128)(2,1)}, u32[]{:S(2)}) copy-start(bf16[128,1024]{1,0:T(8,128)(2,1)} %get-tuple-element.47) | copy-start | bytes 786436
  136.9 5.9 %copy-start.9 = (bf16[128,1024]{1,0:T(8,128)(2,1)S(1)}, bf16[128,1024]{1,0:T(8,128)(2,1)}, u32[]{:S(2)}) copy-start(bf16[128,1024]{1,0:T(8,128)(2,1)} %get-tuple-element.48) | copy-start | bytes 786436
  136.9 7.2 %copy-start.3 = (bf16[256,1024]{1,0:T(8,128)(2,1)S(1)}, bf16[256,1024]{1,0:T(8,128)(2,1)}, u32[]{:S(2)}) copy-start(bf16[256,1024]{1,0:T(8,128)(2,1)} %get-tuple-element.42.x_ref) | copy-start | bytes 1572868
  136.9 7.2 %copy-start.11 = (bf16[1024,2048]{1,0:T(8,128)(2,1)S(1)}, bf16[1024,2048]{1,0:T(8,128)(2,1)}, u32[]{:S(2)}) copy-start(bf16[1024,2048]{1,0:T(8,128)(2,1)} %param.13) | copy-start | bytes 12582916
  136.9 9.4 %collective-permute-start.4 = (bf16[256,512]{1,0:T(8,128)(2,1)S(1)}, bf16[256,512]{1,0:T(8,128)(2,1)S(1)}, u32[]{:S(2)}, u32[]{:S(2)}) collective-permute-start(bf16[256,512]{1,0:T(8,128)(2,1)S(1)} %get-tuple-element.84), channel_id=1, source_target_pairs={{0,1},{1,0},{2,3},{3,2},{4,5},{5,4},{6,7},{7,6},{8,9},{9,8},{10,11... | collective-permute-start | bytes 786440 | tf_op jit(solution)/shard_map/ppermute | solution.py:269
  142.8 101.9 %collective-permute-start.3 = (bf16[128,2048]{1,0:T(8,128)(2,1)S(1)}, bf16[128,2048]{1,0:T(8,128)(2,1)}, u32[]{:S(2)}, u32[]{:S(2)}) collective-permute-start(bf16[128,2048]{1,0:T(8,128)(2,1)S(1)} %pad_maximum_fusion.3), channel_id=1, source_target_pairs={{4,0},{8,4},{12,8},{16,12},{20,16},{24,20},{28,24},{5,1},{9,5},{13... | collective-permute-start | bytes 1572872 | tf_op jit(solution)/shard_map/ppermute | solution.py:23
  253.7 1.7 copy-start.4
  255.4 4.3 %copy-start.5 = (bf16[2048,1024]{1,0:T(8,128)(2,1)S(1)}, bf16[2048,1024]{1,0:T(8,128)(2,1)}, u32[]{:S(2)}) copy-start(bf16[2048,1024]{1,0:T(8,128)(2,1)} %param.11) | copy-start | bytes 12582916
  255.4 4.3 %copy-start.6 = (f32[256,2048]{1,0:T(8,128)S(1)}, f32[256,2048]{1,0:T(8,128)}, u32[]{:S(2)}) copy-start(f32[256,2048]{1,0:T(8,128)} %fusion.17) | copy-start | bytes 6291460
  258.5 20.0 %collective-permute-start.7 = (bf16[256,512]{1,0:T(8,128)(2,1)}, bf16[256,512]{1,0:T(8,128)(2,1)}, u32[]{:S(2)}, u32[]{:S(2)}) collective-permute-start(bf16[256,512]{1,0:T(8,128)(2,1)} %get-tuple-element.80), channel_id=1, source_target_pairs={{0,1},{1,0},{2,3},{3,2},{4,5},{5,4},{6,7},{7,6},{8,9},{9,8},{10,11... | collective-permute-start | bytes 786440 | tf_op jit(solution)/shard_map/ppermute | solution.py:269
  259.6 2.2 copy-start.13
  259.6 22.8 %collective-permute-start.6 = (bf16[256,512]{1,0:T(8,128)(2,1)}, bf16[256,512]{1,0:T(8,128)(2,1)S(1)}, u32[]{:S(2)}, u32[]{:S(2)}) collective-permute-start(bf16[256,512]{1,0:T(8,128)(2,1)} %get-tuple-element.82), channel_id=1, source_target_pairs={{0,1},{1,0},{2,3},{3,2},{4,5},{5,4},{6,7},{7,6},{8,9},{9,8},{10,11... | collective-permute-start | bytes 786440 | tf_op jit(solution)/shard_map/ppermute | solution.py:269
  271.2 7.3 %copy-start.2 = (bf16[256,2048]{1,0:T(8,128)(2,1)S(1)}, bf16[256,2048]{1,0:T(8,128)(2,1)}, u32[]{:S(2)}) copy-start(bf16[256,2048]{1,0:T(8,128)(2,1)} %copy-done.1) | copy-start | bytes 3145732

commit v4 on v3

--- a/solution.py
+++ b/solution.py
@@ -239,7 +239,7 @@
     cubes = [p.reshape((blocks,) + s) for p, s in zip(parts, shapes)]
     sem = pltpu.SemaphoreType.DMA
     outs = pl.pallas_call(
-        functools.partial(reduce_kernel, n_tm, n_roll, call_id == 0),
+        functools.partial(reduce_kernel, n_tm, n_roll, True),
         out_shape=[jax.ShapeDtypeStruct((n_roll,) + s, half) for s in shapes],
         in_specs=[pl.BlockSpec(memory_space=pl.ANY)] * 4,
         out_specs=[pl.BlockSpec(memory_space=pltpu.VMEM)] * 4,

time: 356 us -> 358 us (level)
  no operation moved by 1% of the time
where the time goes in v4:
time: 358 us; the launch traced here: 357 us
  Pallas kernels  200 us (56%)
  waiting for transfers between devices  46.5 us (13%)
  local copies, waits for them, and re-layouts  40.6 us (11%)
  matrix products  28.9 us (8%)
  starting transfers between devices  27.3 us (8%)
  other arithmetic  13 us (4%)
    pallas_call x2, Pallas kernels, reduce_all(): pl.pallas_call(functools.partial(reduce_kernel, n_tm, n_roll, True), out_...  161 us
    all_to_all x1, waiting for transfers between devices, local(): lax.all_to_all(outgoing, 'tm', split_axis=0, concat_axis=0, tiled=True)  32.2 us
    pallas_call x1, Pallas kernels, attend(): pl.pallas_call(attend_kernel, grid=(heads,), in_specs=[column(rows), colu...  17.3 us
    all_to_all x1, starting transfers between devices, local(): lax.all_to_all(slot_grad, 'tm', split_axis=0, concat_axis=0, tiled=True)  14.3 us
    ppermute x2, waiting for transfers between devices, from_behind(): return lax.ppermute(block, axis, route)  14.2 us
    dot_general x4, matrix products, dot_last(): lax.dot_general(left, right, (((1,), (1,)), ((), ())), preferred_element_...  13.4 us
    pallas_call x4, Pallas kernels, partial_halves(): pl.pallas_call(partial_kernel, grid=(depth // tile,), in_specs=[left_spec...  11.8 us
    convert_element_type x9, local copies, waits for them, and re-layouts, assembled(): both.transpose(0, 2, 1, 3).reshape(n_roll // 2 * rows, 4 * width)  11.4 us
  transfers between devices with their start and end apart: 10, of which 2 were waited for; matrix products, arithmetic and copies ran while one was open for 13% of the time, Pallas kernels for 29%

profile of v4, /device:TPU:0, one launch (start us, length us, event | category | flops | bytes accessed | tf_op | source)
XLA Modules:
  0.0 357.2 jit_solution(8387539824885866675)
XLA Ops:
  0.6 9.8 %gather_lists.1 = s32[8,8,8]{2,1,0:T(8,128)} custom-call(s32[8,8]{1,0:T(8,128)} %bitcast.115), custom_call_target="tpu_custom_call" | custom-call | tf_op jit(solution)/shard_map/gather_lists/pallas_call | solution.py:339
  11.7 3.8 %convolution_convert_fusion.4.ko_ref = bf16[256,1024]{1,0:T(8,128)(2,1)S(1)} fusion(bf16[256,2048]{1,0:T(8,128)(2,1)} %bitcast.89, bf16[2048,1024]{1,0:T(8,128)(2,1)} %param.11), kind=kOutput, calls=%fused_computation.10 | convolution fusion | flops 1074003968 | bytes 5767168 | tf_op jit(solution)/shard_map/dot_general | solution.py:363
  18.3 2.1 convolution_convert_fusion.3.vo_ref
  23.1 2.0 pad_maximum_fusion
  25.1 5.5 %all-to-all-start = ((bf16[8,3,32,2048]{3,2,1,0:T(8,128)(2,1)}), bf16[8,3,32,2048]{3,2,1,0:T(8,128)(2,1)}, u32[]{:S(2)}, u32[]{:S(2)}) async-start(bf16[8,3,32,2048]{3,2,1,0:T(8,128)(2,1)} %pad_maximum_fusion), calls=%async_computation | async-start | bytes 6291456 | tf_op jit(solution)/shard_map/all_to_all | solution.py:427
  30.7 2.1 constant_dynamic-slice_fusion.4
  35.1 4.6 %collective-permute-start = (bf16[128,2048]{1,0:T(8,128)(2,1)}, bf16[128,2048]{1,0:T(8,128)(2,1)}, u32[]{:S(2)}, u32[]{:S(2)}) collective-permute-start(bf16[128,2048]{1,0:T(8,128)(2,1)} %pad_maximum_fusion.2), channel_id=1, source_target_pairs={{0,4},{4,8},{8,12},{12,16},{16,20},{20,24},{24,28},{1,5},{5,9},{9,... | collective-permute-start | bytes 1572872 | tf_op jit(solution)/shard_map/ppermute | solution.py:23
  40.8 4.2 %convolution_convert_fusion.6.q_ref = bf16[256,1024]{1,0:T(8,128)(2,1)} fusion(bf16[256,2048]{1,0:T(8,128)(2,1)S(1)} %bitcast.92, bf16[2048,1024]{1,0:T(8,128)(2,1)} %param.10), kind=kOutput, calls=%fused_computation.12 | convolution fusion | flops 1074003968 | bytes 5767168 | tf_op jit(solution)/shard_map/dot_general | solution.py:362
  46.6 2.6 copy.73.bias_ref
  49.2 4.6 %convolution_convert_fusion.5.g_ref = bf16[256,1024]{1,0:T(8,128)(2,1)} fusion(bf16[256,2048]{1,0:T(8,128)(2,1)} %bitcast.114, bf16[1024,2048]{1,0:T(8,128)(2,1)} %param.13), kind=kOutput, calls=%fused_computation.11 | convolution fusion | flops 1074003968 | bytes 5767168 | tf_op jit(solution)/shard_map/dot_general | solution.py:27
  53.8 14.2 %collective-permute-done.kb_ref.vb_ref = bf16[128,2048]{1,0:T(8,128)(2,1)} collective-permute-done((bf16[128,2048]{1,0:T(8,128)(2,1)}, bf16[128,2048]{1,0:T(8,128)(2,1)}, u32[]{:S(2)}, u32[]{:S(2)}) %collective-permute-start) | collective-permute-done | bytes 524320 | tf_op jit(solution)/shard_map/ppermute | solution.py:23
  68.0 32.2 %all-to-all-done = bf16[8,3,32,2048]{3,2,1,0:T(8,128)(2,1)} async-done(((bf16[8,3,32,2048]{3,2,1,0:T(8,128)(2,1)}), bf16[8,3,32,2048]{3,2,1,0:T(8,128)(2,1)}, u32[]{:S(2)}, u32[]{:S(2)}) %all-to-all-start) | async-done | bytes 3145760 | tf_op jit(solution)/shard_map/all_to_all | solution.py:427
  100.3 17.3 %attend.1 = (bf16[256,1024]{1,0:T(8,128)(2,1)}, bf16[256,1024]{1,0:T(8,128)(2,1)}, f32[256,1024]{1,0:T(8,128)}, f32[256,1024]{1,0:T(8,128)}, bf16[128,1024]{1,0:...) custom-call(bf16[256,1024]{1,0:T(8,128)(2,1)} %convolution_convert_fusion.6.q_ref, ...), custom_call_target="tpu_custom_call" | custom-call | flops 3623878656 | bytes 9437184 | tf_op jit(solution)/shard_map/attend/pallas_call | solution.py:77
  117.6 3.9 %pad_maximum_fusion.1 = bf16[768,2048]{1,0:T(8,128)(2,1)} fusion(bf16[768,1024]{1,0:T(8,128)(2,1)} %get-tuple-element.46, bf16[768,1024]{1,0:T(8,128)(2,1)} %get-tuple-element.45), kind=kLoop, calls=%fused_computation.4 | loop fusion | flops 6291456 | bytes 6291456 | tf_op jit(solution)/shard_map/concatenate | solution.py:437
  121.5 14.3 %all-to-all-start.1 = ((bf16[8,3,32,2048]{3,2,1,0:T(8,128)(2,1)}), bf16[8,3,32,2048]{3,2,1,0:T(8,128)(2,1)}, u32[]{:S(2)}, u32[]{:S(2)}) async-start(bf16[8,3,32,2048]{3,2,1,0:T(8,128)(2,1)} %bitcast.96), calls=%async_computation.1 | async-start | bytes 6291456 | tf_op jit(solution)/shard_map/all_to_all | solution.py:438
  137.5 5.3 %fusion.17 = f32[256,2048]{1,0:T(8,128)} fusion(bf16[256,1024]{1,0:T(8,128)(2,1)} %get-tuple-element.43, bf16[2048,1024]{1,0:T(8,128)(2,1)} %param.10), kind=kOutput, calls=%fused_computation.63 | convolution fusion | flops 1073741824 | bytes 6815744 | tf_op jit(solution)/shard_map/dot_general | solution.py:27
  144.1 2.2 convolution_convert_fusion.2
  146.4 3.0 partial_halves.4
  149.3 2.0 partial_halves.5
  151.4 93.3 %reduce_all.2 = (bf16[4,128,256]{2,1,0:T(8,128)(2,1)S(1)}, bf16[4,128,256]{2,1,0:T(8,128)(2,1)S(1)}, bf16[4,64,512]{2,1,0:T(8,128)(2,1)S(1)}, bf16[4,64,512]{2,1,0:T(8,128)(2,1)S(1)}) custom-call(bf16[16,128,256]{2,1,0:T(8,128)(2,1)S(1)} %bitcast.73, bf16[16,128,256]{2,1,0:T(8,128)(2,1)S(1)} %bitcast.74, bf16[16,64,512]{2,1,0:T(8,128)(2,1)S(1)} %bitcast.77, ...), custom_call_target="tpu_custom_call" | custom-call | bytes 167772160 | tf_op jit(solution)/shard_map/reduce_all/pallas_call | solution.py:241
  244.8 3.6 %copy.74 = bf16[8,3,32,2048]{3,0,2,1:T(8,128)(2,1)S(1)} copy(bf16[8,3,32,2048]{3,2,1,0:T(8,128)(2,1)} %all-to-all-done.1) | data formatting | bytes 6291456 | tf_op jit(solution)/shard_map/optimization_barrier | solution.py:446
  248.4 2.0 convolution_bitcast_fusion
  250.4 3.3 reshape.210
  255.4 2.3 fusion.1
  261.8 2.3 fusion
  266.8 2.0 copy.82
  271.2 2.6 copy.75
  273.8 2.2 copy.76
  276.1 2.4 copy.85
  278.5 3.9 %partial_halves.7 = (bf16[2048,256]{1,0:T(8,128)(2,1)S(1)}, bf16[2048,256]{1,0:T(8,128)(2,1)S(1)}) custom-call(bf16[256,2048]{1,0:T(8,128)(2,1)S(1)} %bitcast.94, bf16[256,2048]{1,0:T(8,128)(2,1)S(1)} %copy-done.2, bf16[256,512]{1,0:T(8,128)(2,1)S(1)} %get-tuple-element.81.g_ref, bf16[256,512]{1,0:T(8,128)(2,1)} %collective-permute-done.7.h_ref), custom_call_target="tpu_custom_call" | custom-call | flops 1073741824 | bytes 4718592 | tf_op jit(solution)/shard_map/partial_halves/pallas_call | solution.py:296
  282.4 3.0 partial_halves.6
  285.3 67.5 %reduce_all.3 = (bf16[4,128,256]{2,1,0:T(8,128)(2,1)S(1)}, bf16[4,128,256]{2,1,0:T(8,128)(2,1)S(1)}, bf16[4,128,256]{2,1,0:T(8,128)(2,1)S(1)}, bf16[4,128,256]{2,1,0:T(8,128)(2,1)S(1)}) custom-call(bf16[16,128,256]{2,1,0:T(8,128)(2,1)S(1)} %bitcast.79, bf16[16,128,256]{2,1,0:T(8,128)(2,1)S(1)} %bitcast.80, bf16[16,128,256]{2,1,0:T(8,128)(2,1)S(1)} %bitcast.75, ...), custom_call_target="tpu_custom_call" | custom-call | bytes 167772160 | tf_op jit(solution)/shard_map/reduce_all/pallas_call | solution.py:241
  (101 shorter events, 29.9 us)
Async XLA Ops:
  15.5 1.1 copy-start.7
  15.5 2.0 copy-start
  16.0 2.3 copy-start.12
  25.1 75.1 %all-to-all-start = ((bf16[8,3,32,2048]{3,2,1,0:T(8,128)(2,1)}), bf16[8,3,32,2048]{3,2,1,0:T(8,128)(2,1)}, u32[]{:S(2)}, u32[]{:S(2)}) async-start(bf16[8,3,32,2048]{3,2,1,0:T(8,128)(2,1)} %pad_maximum_fusion), calls=%async_computation | async-start | bytes 6291456 | tf_op jit(solution)/shard_map/all_to_all | solution.py:427
  30.6 3.6 %slice-start = ((bf16[256,1024]{1,0:T(8,128)(2,1)}), bf16[128,1024]{1,0:T(8,128)(2,1)S(1)}, s32[]{:S(2)}) async-start(bf16[256,1024]{1,0:T(8,128)(2,1)} %copy-done.7), calls=%async_computation.2 | async-start | bytes 524288 | tf_op jit(solution)/shard_map/slice | solution.py:375
  30.6 9.1 %copy-start.10 = (s32[1,8,8]{2,1,0:T(8,128)S(1)}, s32[1,8,8]{2,1,0:T(8,128)}, u32[]{:S(2)}) copy-start(s32[1,8,8]{2,1,0:T(8,128)} %param.9) | copy-start | bytes 772
  30.6 37.4 %collective-permute-start.1 = (bf16[256,2048]{1,0:T(8,128)(2,1)S(1)}, bf16[256,2048]{1,0:T(8,128)(2,1)S(1)}, u32[]{:S(2)}, u32[]{:S(2)}) collective-permute-start(bf16[256,2048]{1,0:T(8,128)(2,1)S(1)} %bitcast.91), channel_id=1, source_target_pairs={{0,1},{1,0},{2,3},{3,2},{4,5},{5,4},{6,7},{7,6},{8,9},{9,8},{10,11... | collective-permute-start | bytes 3145736 | tf_op jit(solution)/shard_map/ppermute | solution.py:269
  32.8 21.0 %collective-permute-start.2 = (bf16[256,1024]{1,0:T(8,128)(2,1)}, bf16[256,1024]{1,0:T(8,128)(2,1)S(1)}, u32[]{:S(2)}, u32[]{:S(2)}) collective-permute-start(bf16[256,1024]{1,0:T(8,128)(2,1)} %get-tuple-element.79), channel_id=1, source_target_pairs={{0,1},{1,0},{2,3},{3,2},{4,5},{5,4},{6,7},{7,6},{8,9},{9,8},{10,11... | collective-permute-start | bytes 1572872 | tf_op jit(solution)/shard_map/ppermute | solution.py:269
  35.1 33.0 %collective-permute-start = (bf16[128,2048]{1,0:T(8,128)(2,1)}, bf16[128,2048]{1,0:T(8,128)(2,1)}, u32[]{:S(2)}, u32[]{:S(2)}) collective-permute-start(bf16[128,2048]{1,0:T(8,128)(2,1)} %pad_maximum_fusion.2), channel_id=1, source_target_pairs={{0,4},{4,8},{8,12},{12,16},{16,20},{20,24},{24,28},{1,5},{5,9},{9,... | collective-permute-start | bytes 1572872 | tf_op jit(solution)/shard_map/ppermute | solution.py:23
  68.0 78.3 %copy-start.1 = (bf16[256,2048]{1,0:T(8,128)(2,1)}, bf16[256,2048]{1,0:T(8,128)(2,1)S(1)}, u32[]{:S(2)}) copy-start(bf16[256,2048]{1,0:T(8,128)(2,1)S(1)} %collective-permute-done.1.y_ref) | copy-start | bytes 3145732
  121.5 123.3 %all-to-all-start.1 = ((bf16[8,3,32,2048]{3,2,1,0:T(8,128)(2,1)}), bf16[8,3,32,2048]{3,2,1,0:T(8,128)(2,1)}, u32[]{:S(2)}, u32[]{:S(2)}) async-start(bf16[8,3,32,2048]{3,2,1,0:T(8,128)(2,1)} %bitcast.96), calls=%async_computation.1 | async-start | bytes 6291456 | tf_op jit(solution)/shard_map/all_to_all | solution.py:438
  135.8 13.5 %collective-permute-start.5 = (bf16[256,1024]{1,0:T(8,128)(2,1)}, bf16[256,1024]{1,0:T(8,128)(2,1)S(1)}, u32[]{:S(2)}, u32[]{:S(2)}) collective-permute-start(bf16[256,1024]{1,0:T(8,128)(2,1)} %get-tuple-element.42.x_ref), channel_id=1, source_target_pairs={{0,1},{1,0},{2,3},{3,2},{4,5},{5,4},{6,7},{7,6},{8,9},{9,8},{10,11... | collective-permute-start | bytes 1572872 | tf_op jit(solution)/shard_map/ppermute | solution.py:269
  136.9 5.9 %copy-start.8 = (bf16[128,1024]{1,0:T(8,128)(2,1)S(1)}, bf16[128,1024]{1,0:T(8,128)(2,1)}, u32[]{:S(2)}) copy-start(bf16[128,1024]{1,0:T(8,128)(2,1)} %get-tuple-element.47) | copy-start | bytes 786436
  136.9 5.9 %copy-start.9 = (bf16[128,1024]{1,0:T(8,128)(2,1)S(1)}, bf16[128,1024]{1,0:T(8,128)(2,1)}, u32[]{:S(2)}) copy-start(bf16[128,1024]{1,0:T(8,128)(2,1)} %get-tuple-element.48) | copy-start | bytes 786436
  136.9 7.2 %copy-start.3 = (bf16[256,1024]{1,0:T(8,128)(2,1)S(1)}, bf16[256,1024]{1,0:T(8,128)(2,1)}, u32[]{:S(2)}) copy-start(bf16[256,1024]{1,0:T(8,128)(2,1)} %get-tuple-element.42.x_ref) | copy-start | bytes 1572868
  136.9 7.2 %copy-start.11 = (bf16[1024,2048]{1,0:T(8,128)(2,1)S(1)}, bf16[1024,2048]{1,0:T(8,128)(2,1)}, u32[]{:S(2)}) copy-start(bf16[1024,2048]{1,0:T(8,128)(2,1)} %param.13) | copy-start | bytes 12582916
  136.9 9.4 %collective-permute-start.4 = (bf16[256,512]{1,0:T(8,128)(2,1)S(1)}, bf16[256,512]{1,0:T(8,128)(2,1)S(1)}, u32[]{:S(2)}, u32[]{:S(2)}) collective-permute-start(bf16[256,512]{1,0:T(8,128)(2,1)S(1)} %get-tuple-element.84), channel_id=1, source_target_pairs={{0,1},{1,0},{2,3},{3,2},{4,5},{5,4},{6,7},{7,6},{8,9},{9,8},{10,11... | collective-permute-start | bytes 786440 | tf_op jit(solution)/shard_map/ppermute | solution.py:269
  142.8 101.9 %collective-permute-start.3 = (bf16[128,2048]{1,0:T(8,128)(2,1)S(1)}, bf16[128,2048]{1,0:T(8,128)(2,1)}, u32[]{:S(2)}, u32[]{:S(2)}) collective-permute-start(bf16[128,2048]{1,0:T(8,128)(2,1)S(1)} %pad_maximum_fusion.3), channel_id=1, source_target_pairs={{4,0},{8,4},{12,8},{16,12},{20,16},{24,20},{28,24},{5,1},{9,5},{13... | collective-permute-start | bytes 1572872 | tf_op jit(solution)/shard_map/ppermute | solution.py:23
  253.7 1.7 copy-start.4
  255.4 4.3 %copy-start.5 = (bf16[2048,1024]{1,0:T(8,128)(2,1)S(1)}, bf16[2048,1024]{1,0:T(8,128)(2,1)}, u32[]{:S(2)}) copy-start(bf16[2048,1024]{1,0:T(8,128)(2,1)} %param.11) | copy-start | bytes 12582916
  255.4 4.3 %copy-start.6 = (f32[256,2048]{1,0:T(8,128)S(1)}, f32[256,2048]{1,0:T(8,128)}, u32[]{:S(2)}) copy-start(f32[256,2048]{1,0:T(8,128)} %fusion.17) | copy-start | bytes 6291460
  258.5 20.0 %collective-permute-start.7 = (bf16[256,512]{1,0:T(8,128)(2,1)}, bf16[256,512]{1,0:T(8,128)(2,1)}, u32[]{:S(2)}, u32[]{:S(2)}) collective-permute-start(bf16[256,512]{1,0:T(8,128)(2,1)} %get-tuple-element.80), channel_id=1, source_target_pairs={{0,1},{1,0},{2,3},{3,2},{4,5},{5,4},{6,7},{7,6},{8,9},{9,8},{10,11... | collective-permute-start | bytes 786440 | tf_op jit(solution)/shard_map/ppermute | solution.py:269
  259.6 2.2 copy-start.13
  259.6 22.8 %collective-permute-start.6 = (bf16[256,512]{1,0:T(8,128)(2,1)}, bf16[256,512]{1,0:T(8,128)(2,1)S(1)}, u32[]{:S(2)}, u32[]{:S(2)}) collective-permute-start(bf16[256,512]{1,0:T(8,128)(2,1)} %get-tuple-element.82), channel_id=1, source_target_pairs={{0,1},{1,0},{2,3},{3,2},{4,5},{5,4},{6,7},{7,6},{8,9},{9,8},{10,11... | collective-permute-start | bytes 786440 | tf_op jit(solution)/shard_map/ppermute | solution.py:269
  271.2 7.3 %copy-start.2 = (bf16[256,2048]{1,0:T(8,128)(2,1)S(1)}, bf16[256,2048]{1,0:T(8,128)(2,1)}, u32[]{:S(2)}) copy-start(bf16[256,2048]{1,0:T(8,128)(2,1)} %copy-done.1) | copy-start | bytes 3145732
